TPU v7x, 32 devices: a whole 2x2x4 slice. The times are simulated.
32 devices in a mesh: grp: 2 (over y), site: 4 (over x, core), spin: 4 (over z).
Axes of the slice: x: 2, y: 2, z: 4, core: 2. Of those that a mesh axis runs over, the one named last changes fastest.
Arguments:
- walkers: bfloat16 [8, 512, 256, 256], P(('grp', 'spin'), 'site'), parts along dimension 0, may hold values from -90 to 90
- fields: bfloat16 [8, 1, 512, 256], P(('grp', 'spin'), None, 'site'), parts along dimension 0, may hold values from -3 to 3
- kinetic_x: bfloat16 [512, 512], replicated, may hold values from -0.5 to 1.5
- kinetic_y: bfloat16 [256, 256], replicated, may hold values from -0.5 to 1.5
Outputs:
- orthonormal: bfloat16 [8, 512, 256, 256], P(('grp', 'spin'), 'site'), parts along dimension 0
- triangle: float32 [8, 256, 256], P(('grp', 'spin')), parts along dimension 0
There are 2 independent parts, one for each index of `grp`. A program takes and returns all parts, laid end to end along the dimension named above; an argument that names none is the same for every part. Nothing has to cross between parts.
All inputs are finite; a program needn't handle non-finite values.
Results may differ from a plain program's by a relative error of at most 0.0095.
Values may be sent and summed in bfloat16 or wider, within the bound.
A program may use at most 128 MiB of HBM per device.

v0:
```python
import functools

import jax
import jax.numpy as jnp
from jax import lax
from jax.experimental import pallas as pl
from jax.experimental.pallas import tpu as pltpu
from jax.sharding import PartitionSpec as P

CORES = 2
LANES = 128
TILE = 16
CHUNKS = 4
UNROLL = 8
LINES = 4
VMEM = 48 * 1024 * 1024


def put(acc, row, value):
    for lane in range(acc.shape[0]):
        acc[lane, row : row + value.shape[0], :] = value[:, lane * LANES : (lane + 1) * LANES]


def take(acc, row, count, stride, out, place):
    for lane in range(acc.shape[0]):
        out[place, :, lane * LANES : (lane + 1) * LANES] = acc[
            lane, pl.ds(row, count, stride=stride), :
        ].astype(jnp.bfloat16)


def y_body(parts, rows, sites, base_ref, *refs):
    kinetic, w_ref, outs, acc = refs[:parts], refs[parts], refs[-parts - 1 : -1], refs[-1]
    every = parts * rows
    left = jnp.concatenate([k[...] for k in kinetic], axis=0)

    for x in range(sites):
        put(acc, x * every, jnp.dot(left, w_ref[x], preferred_element_type=jnp.float32))

    for part in range(parts):

        @pl.loop(0, rows, step=UNROLL)
        def _(first, part=part):
            for y in range(UNROLL):
                take(acc, part * rows + first + y, sites, every, outs[part], first + y)


def apply_y(walker, kinetic, bases, rows, after):
    own, depth, orbitals = walker.shape
    parts = len(bases)
    every = rows * parts
    specs = [pl.BlockSpec((rows, depth), lambda i, b, p=p: (b[p], 0)) for p in range(parts)]
    specs.append(pl.BlockSpec((TILE, depth, orbitals), lambda i, b: (i, 0, 0)))
    operands = [kinetic] * parts + [walker]
    if after is not None:
        specs.append(pl.BlockSpec(memory_space=pl.ANY))
        operands.append(after)
    return pl.pallas_call(
        functools.partial(y_body, parts, rows, TILE),
        grid_spec=pltpu.PrefetchScalarGridSpec(
            num_scalar_prefetch=1,
            grid=(own // TILE,),
            in_specs=specs,
            out_specs=[pl.BlockSpec((rows, TILE, orbitals), lambda i, b: (0, i, 0))] * parts,
            scratch_shapes=[pltpu.VMEM((orbitals // LANES, TILE * every, LANES), jnp.float32)],
        ),
        out_shape=[jax.ShapeDtypeStruct((rows, own, orbitals), jnp.bfloat16)] * parts,
        compiler_params=pltpu.CompilerParams(vmem_limit_bytes=VMEM),
        cost_estimate=pl.CostEstimate(
            flops=2 * every * own * depth * orbitals,
            bytes_accessed=2 * own * orbitals * (depth + every),
            transcendentals=0,
        ),
        name="apply_y",
    )(jnp.stack(bases) // rows, *operands)


def x_body(count, lines, own, k_ref, f_ref, g_ref, *refs):
    ins, outs, gram = refs[:count], refs[count : 2 * count], refs[2 * count]

    @pl.when(pl.program_id(0) == 0)
    def _():
        gram[...] = g_ref[...]

    total = None
    for y in range(lines):
        column = jnp.concatenate([r[y] for r in ins], axis=0)
        moved = jnp.dot(k_ref[...], column, preferred_element_type=jnp.float32)
        factor = f_ref[0, :, y : y + 1]
        out = (factor * moved.astype(jnp.bfloat16).astype(jnp.float32)).astype(jnp.bfloat16)
        for e in range(count):
            outs[e][y] = out[e * own : (e + 1) * own]
        part = lax.dot_general(out, out, (((0,), (0,)), ((), ())), preferred_element_type=jnp.float32)
        total = part if total is None else total + part
    gram[...] += total


def apply_x(columns, kinetic, factor, gram, lines):
    count = len(columns)
    rows, own, orbitals = columns[0].shape
    every = count * own
    block = pl.BlockSpec((lines, own, orbitals), lambda i: (i, 0, 0))
    outs = pl.pallas_call(
        functools.partial(x_body, count, lines, own),
        grid=(rows // lines,),
        in_specs=[
            pl.BlockSpec((every, every), lambda i: (0, 0)),
            pl.BlockSpec((1, every, lines), lambda i: (i, 0, 0)),
            pl.BlockSpec((orbitals, orbitals), lambda i: (0, 0)),
        ]
        + [block] * count,
        out_specs=[block] * count + [pl.BlockSpec((orbitals, orbitals), lambda i: (0, 0))],
        out_shape=[jax.ShapeDtypeStruct((rows, own, orbitals), jnp.bfloat16)] * count
        + [jax.ShapeDtypeStruct((orbitals, orbitals), jnp.float32)],
        compiler_params=pltpu.CompilerParams(vmem_limit_bytes=VMEM),
        cost_estimate=pl.CostEstimate(
            flops=2 * rows * every * orbitals * (every + orbitals),
            bytes_accessed=4 * rows * every * orbitals,
            transcendentals=0,
        ),
        name="apply_x",
    )(kinetic, factor, gram, *columns)
    return outs[:count], outs[count]


def out_body(parts, steps, lines, sites, base_ref, *refs):
    ins, v_ref, out, held, acc = refs[:parts], refs[parts], refs[-3], refs[-2], refs[-1]
    for p in range(parts):

        @pl.when(pl.program_id(0) // steps == p)
        def _(p=p):
            held[...] = ins[p][...]

    @pl.loop(0, lines, step=4)
    def _(first):
        for y in range(4):
            row = pl.multiple_of((first + y) * sites, sites)
            value = jnp.dot(held[first + y], v_ref[...], preferred_element_type=jnp.float32)
            for lane in range(acc.shape[0]):
                acc[lane, pl.ds(row, sites), :] = value[:, lane * LANES : (lane + 1) * LANES]

    @pl.loop(0, sites, step=UNROLL)
    def _(first):
        for x in range(UNROLL):
            take(acc, first + x, lines, sites, out, first + x)


def orthonormal_rows(pieces, inverse, bases, result, shape):
    parts = len(pieces)
    rows, own, orbitals = pieces[0].shape
    lines, sites = TILE, min(own, 32)
    across = own // sites
    steps = (rows // lines) * across

    def piece_at(p):
        def at(i, b):
            j = jnp.clip(i - p * steps, 0, steps - 1)
            return (j // across, j % across, 0)

        return at

    def out_at(i, b):
        j = i % steps
        return (j % across, b[i // steps] + j // across, 0)

    specs = [pl.BlockSpec((lines, sites, orbitals), piece_at(p)) for p in range(parts)]
    specs.append(pl.BlockSpec((orbitals, orbitals), lambda i, b: (0, 0)))
    operands = [*pieces, inverse]
    aliases = {}
    if result is not None:
        specs.append(pl.BlockSpec(memory_space=pl.ANY))
        operands.append(result)
        aliases = {parts + 2: 0}
    return pl.pallas_call(
        functools.partial(out_body, parts, steps, lines, sites),
        grid_spec=pltpu.PrefetchScalarGridSpec(
            num_scalar_prefetch=1,
            grid=(parts * steps,),
            in_specs=specs,
            out_specs=pl.BlockSpec((sites, lines, orbitals), out_at),
            scratch_shapes=[
                pltpu.VMEM((lines, sites, orbitals), jnp.bfloat16),
                pltpu.VMEM((orbitals // LANES, lines * sites, LANES), jnp.float32),
            ],
        ),
        out_shape=jax.ShapeDtypeStruct(shape, jnp.bfloat16),
        input_output_aliases=aliases,
        compiler_params=pltpu.CompilerParams(vmem_limit_bytes=VMEM),
        cost_estimate=pl.CostEstimate(
            flops=2 * parts * rows * own * orbitals * orbitals,
            bytes_accessed=4 * parts * rows * own * orbitals,
            transcendentals=0,
        ),
        name="orthonormal_rows",
    )(jnp.stack(bases) // lines, *operands)


def times(left, right):
    return jnp.dot(left, right, precision=lax.Precision.HIGHEST, preferred_element_type=jnp.float32)


def small_inverse(lower):
    identity = jnp.eye(lower.shape[-1], dtype=jnp.float32)
    return jax.scipy.linalg.solve_triangular(lower, identity, lower=True)


def factorize(gram):
    half = gram.shape[-1] // 2
    upper = jnp.zeros((half, half), jnp.float32)
    first = jnp.linalg.cholesky(gram[:half, :half])
    first_inverse = small_inverse(first)
    below = times(gram[half:, :half], first_inverse.T)
    second = jnp.linalg.cholesky(gram[half:, half:] - times(below, below.T))
    second_inverse = small_inverse(second)
    corner = -times(second_inverse, times(below, first_inverse))
    lower = jnp.block([[first, upper], [below, second]])
    inverse = jnp.block([[first_inverse.T, corner.T], [upper, second_inverse.T]])
    return lower, inverse.astype(jnp.bfloat16)


def one_walker(count, walker, field, kinetic_x, kinetic_y):
    me = lax.axis_index("site")
    own, depth, orbitals = walker.shape
    share = depth // count
    chunks = max(1, min(CHUNKS, share // TILE))
    rows = share // chunks
    lines = min(LINES, rows)
    far = [d for d in range(count) if d >= CORES]
    near = [d for d in range(count) if d < CORES]

    def swap(value, d):
        if d == 0:
            return value
        return lax.ppermute(value, "site", [(s, s ^ d) for s in range(count)])

    def base(d, c):
        return (me ^ d) * share + c * rows

    blocks = [[None] * count for _ in range(chunks)]
    sent = [None]
    for c in range(chunks):
        sent = apply_y(walker, kinetic_y, [base(d, c) for d in far], rows, sent[0])
        for d, value in zip(far, sent):
            blocks[c][d] = swap(value, d)
    pairs = [(d, c) for c in range(chunks) for d in near]
    sent = apply_y(walker, kinetic_y, [base(d, c) for d, c in pairs], rows, sent[0])
    for (d, c), value in zip(pairs, sent):
        blocks[c][d] = swap(value, d)

    fields = [
        swap(lax.dynamic_slice_in_dim(field, (me ^ d) * share, share, 1), d)
        for d in range(count)
    ]
    order = [
        lax.dynamic_slice_in_dim(kinetic_x, (me ^ d) * own, own, 0) for d in range(count)
    ]
    order = jnp.concatenate(order, axis=0)
    order = jnp.concatenate(
        [lax.dynamic_slice_in_dim(order, (me ^ d) * own, own, 1) for d in range(count)], axis=1
    )
    factor = jnp.exp(jnp.concatenate(fields, axis=0).astype(jnp.float32))
    factor = factor.reshape(count * own, share // lines, lines).swapaxes(0, 1)

    scaled, gram = [], jnp.zeros((orbitals, orbitals), jnp.float32)
    per = rows // lines
    for c in range(chunks):
        outs, gram = apply_x(blocks[c], order, factor[c * per : (c + 1) * per], gram, lines)
        scaled.append(outs)
    gram = gram * (1.0 / (count * own * depth))
    step = 1
    while step < count:
        gram = gram + swap(gram, step)
        step *= 2

    home = [[swap(scaled[c][e], e) for e in range(count)] for c in range(chunks)]
    lower, inverse = factorize(gram)
    pieces = [(c, e) for c in range(chunks) for e in near]
    late = [(c, e) for c in range(chunks) for e in far]
    cut = len(late) // 2
    result = None
    for group in [pieces + late[:cut]] + [[one] for one in late[cut:]]:
        result = orthonormal_rows(
            [home[c][e] for c, e in group], inverse, [base(e, c) for c, e in group], result, walker.shape
        )
    return result, lower


def per_device(count, walkers, fields, kinetic_x, kinetic_y):
    results, lowers = [], []
    for w in range(walkers.shape[0]):
        result, lower = one_walker(count, walkers[w], fields[w, 0], kinetic_x, kinetic_y)
        results.append(result[None])
        lowers.append(lower[None])
    return jnp.concatenate(results, axis=0), jnp.concatenate(lowers, axis=0)


def solution(mesh):
    count = mesh.shape["site"]
    placed = (
        P(("grp", "spin"), "site", None, None),
        P(("grp", "spin"), None, "site", None),
        P(),
        P(),
    )

    def body(walkers, fields, kinetic_x, kinetic_y):
        return per_device(count, walkers, fields, kinetic_x, kinetic_y)

    step = jax.shard_map(
        body,
        mesh=mesh,
        in_specs=placed,
        out_specs=(P(("grp", "spin"), "site", None, None), P(("grp", "spin"), None, None)),
        check_vma=False,
    )

    def whole(walkers, fields, kinetic_x, kinetic_y):
        chunks = max(1, min(CHUNKS, walkers.shape[2] // count // TILE))
        run = step
        if chunks > 1:
            run = step
        return run(walkers, fields, kinetic_x, kinetic_y)

    return whole
```

profile of v0, /device:TPU:0, one launch (start us, length us, event | category | flops | bytes accessed | tf_op | source)
XLA Modules:
  0.0 495.4 jit_solution(8904291878955001198)
XLA Ops:
  1.7 12.3 %apply_y.5 = (bf16[16,128,256]{2,1,0:T(8,128)(2,1)S(1)}, bf16[16,128,256]{2,1,0:T(8,128)(2,1)}) custom-call(s32[2]{0:T(128)S(1)} %get-tuple-element.96.base_ref, bf16[256,256]{1,0:T(8,128)(2,1)S(1)} %copy-done, bf16[256,256]{1,0:T(8,128)(2,1)S(1)} %copy-done, bf16[128,256,256]{2,1,0:T(8,128)(2,1)} %bitcast.59), custom_call_target="tpu_custom_call" | custom-call | flops 536870912 | bytes 18874368 | tf_op jit(solution)/shard_map/apply_y/pallas_call | solution.py:57
  14.0 11.5 %apply_y.6 = (bf16[16,128,256]{2,1,0:T(8,128)(2,1)S(1)}, bf16[16,128,256]{2,1,0:T(8,128)(2,1)S(1)}) custom-call(s32[2]{0:T(128)S(1)} %get-tuple-element.97.base_ref, bf16[256,256]{1,0:T(8,128)(2,1)S(1)} %copy-done.1, bf16[256,256]{1,0:T(8,128)(2,1)S(1)} %copy-done.1, bf16[128,256,256]{2,1,0:T(8,128)(2,1)} %bitcast.60, ...), custom_call_target="tpu_custom_call" | custom-call | flops 536870912 | bytes 18874368 | tf_op jit(solution)/shard_map/apply_y/pallas_call | solution.py:57
  25.6 1.0 copy-done.22
  26.7 11.5 %apply_y.7 = (bf16[16,128,256]{2,1,0:T(8,128)(2,1)S(1)}, bf16[16,128,256]{2,1,0:T(8,128)(2,1)S(1)}) custom-call(s32[2]{0:T(128)S(1)} %get-tuple-element.98.base_ref, bf16[256,256]{1,0:T(8,128)(2,1)S(1)} %copy-done.1, bf16[256,256]{1,0:T(8,128)(2,1)S(1)} %copy-done.1, bf16[128,256,256]{2,1,0:T(8,128)(2,1)} %bitcast.61, ...), custom_call_target="tpu_custom_call" | custom-call | flops 536870912 | bytes 18874368 | tf_op jit(solution)/shard_map/apply_y/pallas_call | solution.py:57
  38.2 1.0 copy-done.16
  39.2 12.3 %apply_y.8 = (bf16[16,128,256]{2,1,0:T(8,128)(2,1)}, bf16[16,128,256]{2,1,0:T(8,128)(2,1)S(1)}) custom-call(s32[2]{0:T(128)S(1)} %get-tuple-element.99.base_ref, bf16[256,256]{1,0:T(8,128)(2,1)S(1)} %copy-done.1, bf16[256,256]{1,0:T(8,128)(2,1)S(1)} %copy-done.1, bf16[128,256,256]{2,1,0:T(8,128)(2,1)} %bitcast.62, ...), custom_call_target="tpu_custom_call" | custom-call | flops 536870912 | bytes 18874368 | tf_op jit(solution)/shard_map/apply_y/pallas_call | solution.py:57
  52.4 17.7 %apply_y.9 = (bf16[16,128,256]{2,1,0:T(8,128)(2,1)S(1)}, bf16[16,128,256]{2,1,0:T(8,128)(2,1)}, bf16[16,128,256]{2,1,0:T(8,128)(2,1)S(1)}, bf16[16,128,256]{2,1,...) custom-call(s32[8]{0:T(128)S(1)} %and_select_fusion.5.base_ref, ...), custom_call_target="tpu_custom_call" | custom-call | flops 2147483648 | bytes 25165824 | tf_op jit(solution)/shard_map/apply_y/pallas_call | solution.py:57
  70.2 1.0 copy-done.18
  71.1 1.1 copy-done.20
  72.2 1.1 copy-done.21
  73.8 2.5 collective-permute-start.4
  76.7 1.8 collective-permute-start.2
  78.6 44.1 %collective-permute-done.2 = bf16[128,64]{0,1:T(8,128)(2,1)S(1)} collective-permute-done((bf16[128,64]{0,1:T(8,128)(2,1)S(1)}, bf16[128,64]{0,1:T(8,128)(2,1)S(1)}, u32[]{:S(2)}, u32[]{:S(2)}) %collective-permute-start.2) | collective-permute-done | bytes 16416 | tf_op jit(solution)/shard_map/ppermute | solution.py:233
  122.7 1.5 collective-permute-start.1
  124.3 2.2 collective-permute-done.1
  126.4 1.2 collective-permute-done
  127.6 1.5 collective-permute-start.7
  129.9 1.1 constant_dynamic-slice_fusion.11
  131.3 1.5 collective-permute-start.10
  132.9 2.7 copy.40
  135.6 18.2 %collective-permute-done.7.refs_2_ = bf16[16,128,256]{2,1,0:T(8,128)(2,1)} collective-permute-done((bf16[16,128,256]{2,1,0:T(8,128)(2,1)S(1)}, bf16[16,128,256]{2,1,0:T(8,128)(2,1)}, u32[]{:S(2)}, u32[]{:S(2)}) %collective-permute-start.7) | collective-permute-done | bytes 1048608 | tf_op jit(solution)/shard_map/ppermute | solution.py:233
  153.8 1.5 collective-permute-start.13
  155.2 20.0 %collective-permute-done.8.refs_3_ = bf16[16,128,256]{2,1,0:T(8,128)(2,1)} collective-permute-done((bf16[16,128,256]{2,1,0:T(8,128)(2,1)}, bf16[16,128,256]{2,1,0:T(8,128)(2,1)}, u32[]{:S(2)}, u32[]{:S(2)}) %collective-permute-start.8) | collective-permute-done | bytes 1048608 | tf_op jit(solution)/shard_map/ppermute | solution.py:233
  176.1 1.1 collective-permute-start.14
  177.1 4.3 fusion.17
  181.5 6.3 %apply_x.4 = (bf16[16,128,256]{2,1,0:T(8,128)(2,1)S(1)}, bf16[16,128,256]{2,1,0:T(8,128)(2,1)S(1)}, bf16[16,128,256]{2,1,0:T(8,128)(2,1)S(1)}, bf16[16,128,256]{2,1,0:T(8,128)(2,1)S(1)}, f32[256,256]{1,0:T(8,128)S(1)}) custom-call(bf16[512,512]{1,0:T(8,128)(2,1)S(1)} %pad_maximum_fusion.1.k_ref, f32[4,512,4]{2,1,0:T(8,128)} %get-tuple-element.80.f_ref, ...), custom_call_target="tpu_custom_call" | custom-call | flops 3221225472 | bytes 8388608 | tf_op jit(solution)/shard_map/apply_x/pallas_call | solution.py:102
  187.8 1.0 copy-done.11
  189.8 1.1 copy-done.15
  190.9 1.0 copy-done.4
  192.0 6.3 %apply_x.5 = (bf16[16,128,256]{2,1,0:T(8,128)(2,1)S(1)}, bf16[16,128,256]{2,1,0:T(8,128)(2,1)S(1)}, bf16[16,128,256]{2,1,0:T(8,128)(2,1)S(1)}, bf16[16,128,256]{2,1,0:T(8,128)(2,1)S(1)}, f32[256,256]{1,0:T(8,128)S(1)}) custom-call(bf16[512,512]{1,0:T(8,128)(2,1)S(1)} %copy-done.4, f32[4,512,4]{2,1,0:T(8,128)} %get-tuple-element.81.f_ref, ...), custom_call_target="tpu_custom_call" | custom-call | flops 3221225472 | bytes 8388608 | tf_op jit(solution)/shard_map/apply_x/pallas_call | solution.py:102
  198.3 1.0 copy-done.7
  199.3 1.0 copy-done.10
  200.3 1.1 copy-done.17
  201.3 18.8 %collective-permute-done.11.refs_3_ = bf16[16,128,256]{2,1,0:T(8,128)(2,1)} collective-permute-done((bf16[16,128,256]{2,1,0:T(8,128)(2,1)}, bf16[16,128,256]{2,1,0:T(8,128)(2,1)}, u32[]{:S(2)}, u32[]{:S(2)}) %collective-permute-start.11) | collective-permute-done | bytes 1048608 | tf_op jit(solution)/shard_map/ppermute | solution.py:233
  220.2 6.3 %apply_x.6 = (bf16[16,128,256]{2,1,0:T(8,128)(2,1)S(1)}, bf16[16,128,256]{2,1,0:T(8,128)(2,1)S(1)}, bf16[16,128,256]{2,1,0:T(8,128)(2,1)S(1)}, bf16[16,128,256]{2,1,0:T(8,128)(2,1)S(1)}, f32[256,256]{1,0:T(8,128)S(1)}) custom-call(bf16[512,512]{1,0:T(8,128)(2,1)S(1)} %copy-done.4, f32[4,512,4]{2,1,0:T(8,128)} %get-tuple-element.82.f_ref, ...), custom_call_target="tpu_custom_call" | custom-call | flops 3221225472 | bytes 8388608 | tf_op jit(solution)/shard_map/apply_x/pallas_call | solution.py:102
  226.5 1.0 copy-done.5
  227.5 1.0 copy-done.6
  229.4 14.1 %collective-permute-done.13.refs_2_ = bf16[16,128,256]{2,1,0:T(8,128)(2,1)S(1)} collective-permute-done((bf16[16,128,256]{2,1,0:T(8,128)(2,1)}, bf16[16,128,256]{2,1,0:T(8,128)(2,1)S(1)}, u32[]{:S(2)}, u32[]{:S(2)}) %collective-permute-start.13) | collective-permute-done | bytes 1048608 | tf_op jit(solution)/shard_map/ppermute | solution.py:233
  243.5 20.9 %collective-permute-done.14.refs_3_ = bf16[16,128,256]{2,1,0:T(8,128)(2,1)S(1)} collective-permute-done((bf16[16,128,256]{2,1,0:T(8,128)(2,1)}, bf16[16,128,256]{2,1,0:T(8,128)(2,1)S(1)}, u32[]{:S(2)}, u32[]{:S(2)}) %collective-permute-start.14) | collective-permute-done | bytes 1048608 | tf_op jit(solution)/shard_map/ppermute | solution.py:233
  265.4 6.5 %apply_x.7 = (bf16[16,128,256]{2,1,0:T(8,128)(2,1)S(1)}, bf16[16,128,256]{2,1,0:T(8,128)(2,1)S(1)}, bf16[16,128,256]{2,1,0:T(8,128)(2,1)S(1)}, bf16[16,128,256]{2,1,0:T(8,128)(2,1)S(1)}, f32[256,256]{1,0:T(8,128)S(1)}) custom-call(bf16[512,512]{1,0:T(8,128)(2,1)S(1)} %copy-done.4, f32[4,512,4]{2,1,0:T(8,128)} %get-tuple-element.83.f_ref, ...), custom_call_target="tpu_custom_call" | custom-call | flops 3221225472 | bytes 8388608 | tf_op jit(solution)/shard_map/apply_x/pallas_call | solution.py:102
  273.8 1.0 copy-done.9
  278.3 1.2 collective-permute-done.16
  279.5 1.0 fusion.15
  280.4 1.5 collective-permute-start.17
  283.3 5.9 %collective-permute-done.17 = f32[256,256]{0,1:T(8,128)} collective-permute-done((f32[256,256]{0,1:T(8,128)S(1)}, f32[256,256]{0,1:T(8,128)}, u32[]{:S(2)}, u32[]{:S(2)}) %collective-permute-start.17) | collective-permute-done | bytes 262176 | tf_op jit(solution)/shard_map/ppermute | solution.py:233
  289.2 1.5 collective-permute-start.25
  290.7 1.0 add.126
  293.3 11.7 %cholesky.44 = f32[128,128]{1,0:T(8,128)S(1)} custom-call(f32[128,128]{1,0:T(8,128)S(1)} %fusion.13), custom_call_target="Cholesky" | custom-call | tf_op jit(solution)/shard_map/jit(cholesky)/cholesky | solution.py:209
  306.5 9.8 %custom-call.6 = f32[1,128,128]{1,2,0:T(8,128)S(1)} custom-call(f32[1,128,128]{2,1,0:T(8,128)S(1)} %get-tuple-element.78), custom_call_target="InvertDiagBlocksLowerTriangular" | custom-call | tf_op jit(solution)/shard_map/jit(_solve_triangular)/triangular_solve | solution.py:203
  316.6 1.0 fusion.8
  317.8 1.1 slice_subtract_fusion
  319.9 11.7 %cholesky.55 = f32[128,128]{1,0:T(8,128)S(1)} custom-call(f32[128,128]{1,0:T(8,128)S(1)} %fusion.11), custom_call_target="Cholesky" | custom-call | tf_op jit(solution)/shard_map/jit(cholesky)/cholesky | solution.py:212
  333.0 10.6 %custom-call.7 = f32[1,128,128]{1,2,0:T(8,128)} custom-call(f32[1,128,128]{2,1,0:T(8,128)S(1)} %get-tuple-element.76), custom_call_target="InvertDiagBlocksLowerTriangular" | custom-call | tf_op jit(solution)/shard_map/jit(_solve_triangular)/triangular_solve | solution.py:203
  343.6 1.2 collective-permute-start.28
  345.1 1.5 collective-permute-start.18
  347.5 1.1 fusion.4
  349.4 15.4 %collective-permute-done.27.refs_10_ = bf16[16,128,256]{2,1,0:T(8,128)(2,1)} collective-permute-done((bf16[16,128,256]{2,1,0:T(8,128)(2,1)}, bf16[16,128,256]{2,1,0:T(8,128)(2,1)}, u32[]{:S(2)}, u32[]{:S(2)}) %collective-permute-start.27) | collective-permute-done | bytes 1048608 | tf_op jit(solution)/shard_map/ppermute | solution.py:233
  364.8 1.4 collective-permute-start.15
  368.0 20.4 %collective-permute-done.28.refs_11_ = bf16[16,128,256]{2,1,0:T(8,128)(2,1)} collective-permute-done((bf16[16,128,256]{2,1,0:T(8,128)(2,1)}, bf16[16,128,256]{2,1,0:T(8,128)(2,1)}, u32[]{:S(2)}, u32[]{:S(2)}) %collective-permute-start.28) | collective-permute-done | bytes 1048608 | tf_op jit(solution)/shard_map/ppermute | solution.py:233
  388.5 81.9 %orthonormal_rows.5.refs_2_ = bf16[128,256,256]{2,1,0:T(8,128)(2,1)} custom-call(s32[12]{0:T(128)S(1)} %and_select_fusion.base_ref, bf16[16,128,256]{2,1,0:T(8,128)(2,1)S(1)} %get-tuple-element.64.refs_0_, bf16[16,128,256]{2,1,0:T(8,128)(2,1)} %collective-permute-done.21.refs_1_, bf16[16,128,256]{2,1,0:T(8,128)(2,1)S(1)} %get-tuple-element.66.refs_2_, ...), custom_call_target="tpu_custom_call" | custom-call | flops 3221225472 | bytes 25165824 | tf_op jit(solution)/shard_map/orthonormal_rows/pallas_call | solution.py:173
  470.4 6.5 %orthonormal_rows.6.refs_2_ = bf16[128,256,256]{2,1,0:T(8,128)(2,1)} custom-call(s32[1]{0:T(128)S(6)} %select_n.85.base_ref, bf16[16,128,256]{2,1,0:T(8,128)(2,1)} %collective-permute-done.20.refs_0_, bf16[256,256]{1,0:T(8,128)(2,1)S(1)} %fusion.3.refs_12_.refs_1_, bf16[128,256,256]{2,1,0:T(8,128)(2,1)} %orthonormal_rows.5.refs_2_), custom_call_target="tpu_custom_call", output_to_operand_aliasing={{}: (3, {})} | custom-call | flops 268435456 | bytes 2097152 | tf_op jit(solution)/shard_map/orthonormal_rows/pallas_call | solution.py:173
  476.9 6.5 %orthonormal_rows.7.refs_2_ = bf16[128,256,256]{2,1,0:T(8,128)(2,1)} custom-call(s32[1]{0:T(128)S(6)} %select_n.84.base_ref, bf16[16,128,256]{2,1,0:T(8,128)(2,1)} %collective-permute-done.19.refs_0_, bf16[256,256]{1,0:T(8,128)(2,1)S(1)} %fusion.3.refs_12_.refs_1_, bf16[128,256,256]{2,1,0:T(8,128)(2,1)} %orthonormal_rows.6.refs_2_), custom_call_target="tpu_custom_call", output_to_operand_aliasing={{}: (3, {})} | custom-call | flops 268435456 | bytes 2097152 | tf_op jit(solution)/shard_map/orthonormal_rows/pallas_call | solution.py:173
  483.3 6.5 %orthonormal_rows.8.refs_2_ = bf16[128,256,256]{2,1,0:T(8,128)(2,1)} custom-call(s32[1]{0:T(128)S(6)} %select_n.83.base_ref, bf16[16,128,256]{2,1,0:T(8,128)(2,1)} %collective-permute-done.18.refs_0_, bf16[256,256]{1,0:T(8,128)(2,1)S(1)} %fusion.3.refs_12_.refs_1_, bf16[128,256,256]{2,1,0:T(8,128)(2,1)} %orthonormal_rows.7.refs_2_), custom_call_target="tpu_custom_call", output_to_operand_aliasing={{}: (3, {})} | custom-call | flops 268435456 | bytes 2097152 | tf_op jit(solution)/shard_map/orthonormal_rows/pallas_call | solution.py:173
  489.8 5.6 %orthonormal_rows.9 = bf16[128,256,256]{2,1,0:T(8,128)(2,1)} custom-call(s32[1]{0:T(128)S(6)} %select_n.69.base_ref, bf16[16,128,256]{2,1,0:T(8,128)(2,1)S(1)} %collective-permute-done.15.refs_0_, bf16[256,256]{1,0:T(8,128)(2,1)S(1)} %fusion.3.refs_12_.refs_1_, bf16[128,256,256]{2,1,0:T(8,128)(2,1)} %orthonormal_rows.8.refs_2_), custom_call_target="tpu_custom_call", output_to_operand_aliasing={{}: (3, {})} | custom-call | flops 268435456 | bytes 2097152 | tf_op jit(solution)/shard_map/orthonormal_rows/pallas_call | solution.py:173
  (117 shorter events, 24.2 us)
Async XLA Ops:
  0.8 0.9 copy-start
  1.7 12.3 %copy-start.1 = (bf16[256,256]{1,0:T(8,128)(2,1)S(1)}, bf16[256,256]{1,0:T(8,128)(2,1)}, u32[]{:S(2)}) copy-start(bf16[256,256]{1,0:T(8,128)(2,1)} %refs_7_.1) | copy-start | bytes 393220
  25.5 1.0 copy-start.22
  38.2 1.0 copy-start.16
  39.2 37.3 %copy-start.24 = (bf16[1,1,128,256]{3,2,1,0:T(8,128)(2,1)S(1)}, bf16[1,1,128,256]{3,2,1,0:T(8,128)(2,1)}, u32[]{:S(2)}) copy-start(bf16[1,1,128,256]{3,2,1,0:T(8,128)(2,1)} %param.8) | copy-start | bytes 196612
  51.4 1.0 copy-start.13
  70.2 1.0 copy-start.18
  71.1 1.1 copy-start.20
  72.2 1.1 copy-start.21
  73.3 55.8 %collective-permute-start.3 = (bf16[16,128,256]{2,1,0:T(8,128)(2,1)}, bf16[16,128,256]{2,1,0:T(8,128)(2,1)}, u32[]{:S(2)}, u32[]{:S(2)}) collective-permute-start(bf16[16,128,256]{2,1,0:T(8,128)(2,1)} %get-tuple-element.45), channel_id=1, source_target_pairs={{0,4},{4,0},{8,12},{12,8},{1,5},{5,1},{9,13},{13,9},{2,6},{6,2},{1... | collective-permute-start | bytes 3145736 | tf_op jit(solution)/shard_map/ppermute | solution.py:233
  73.8 55.4 %collective-permute-start.4 = (bf16[16,128,256]{2,1,0:T(8,128)(2,1)S(1)}, bf16[16,128,256]{2,1,0:T(8,128)(2,1)}, u32[]{:S(2)}, u32[]{:S(2)}) collective-permute-start(bf16[16,128,256]{2,1,0:T(8,128)(2,1)S(1)} %get-tuple-element.40.refs_3_), channel_id=1, source_target_pairs={{0,8},{4,12},{8,0},{12,4},{1,9},{5,13},{9,1},{13,5},{2,10},{6,14},... | collective-permute-start | bytes 3145736 | tf_op jit(solution)/shard_map/ppermute | solution.py:233
  76.2 55.1 %collective-permute-start.5 = (bf16[16,128,256]{2,1,0:T(8,128)(2,1)}, bf16[16,128,256]{2,1,0:T(8,128)(2,1)}, u32[]{:S(2)}, u32[]{:S(2)}) collective-permute-start(bf16[16,128,256]{2,1,0:T(8,128)(2,1)} %get-tuple-element.46), channel_id=1, source_target_pairs={{0,12},{4,8},{8,4},{12,0},{1,13},{5,9},{9,5},{13,1},{2,14},{6,10},... | collective-permute-start | bytes 3145736 | tf_op jit(solution)/shard_map/ppermute | solution.py:233
  76.4 56.5 %collective-permute-start.6 = (bf16[16,128,256]{2,1,0:T(8,128)(2,1)}, bf16[16,128,256]{2,1,0:T(8,128)(2,1)}, u32[]{:S(2)}, u32[]{:S(2)}) collective-permute-start(bf16[16,128,256]{2,1,0:T(8,128)(2,1)} %get-tuple-element.49), channel_id=1, source_target_pairs={{0,4},{4,0},{8,12},{12,8},{1,5},{5,1},{9,13},{13,9},{2,6},{6,2},{1... | collective-permute-start | bytes 3145736 | tf_op jit(solution)/shard_map/ppermute | solution.py:233
  76.7 46.0 %collective-permute-start.2 = (bf16[128,64]{0,1:T(8,128)(2,1)S(1)}, bf16[128,64]{0,1:T(8,128)(2,1)S(1)}, u32[]{:S(2)}, u32[]{:S(2)}) collective-permute-start(bf16[128,64]{0,1:T(8,128)(2,1)S(1)} %bitcast.69), channel_id=1, source_target_pairs={{0,12},{4,8},{8,4},{12,0},{1,13},{5,9},{9,5},{13,1},{2,14},{6,10},... | collective-permute-start | bytes 49160 | tf_op jit(solution)/shard_map/ppermute | solution.py:233
  122.7 3.7 collective-permute-start.1
  126.4 1.2 collective-permute-start
  127.6 26.1 %collective-permute-start.7 = (bf16[16,128,256]{2,1,0:T(8,128)(2,1)S(1)}, bf16[16,128,256]{2,1,0:T(8,128)(2,1)}, u32[]{:S(2)}, u32[]{:S(2)}) collective-permute-start(bf16[16,128,256]{2,1,0:T(8,128)(2,1)S(1)} %get-tuple-element.41.refs_3_), channel_id=1, source_target_pairs={{0,8},{4,12},{8,0},{12,4},{1,9},{5,13},{9,1},{13,5},{2,10},{6,14},... | collective-permute-start | bytes 3145736 | tf_op jit(solution)/shard_map/ppermute | solution.py:233
  129.1 46.1 %collective-permute-start.8 = (bf16[16,128,256]{2,1,0:T(8,128)(2,1)}, bf16[16,128,256]{2,1,0:T(8,128)(2,1)}, u32[]{:S(2)}, u32[]{:S(2)}) collective-permute-start(bf16[16,128,256]{2,1,0:T(8,128)(2,1)} %copy-done.22), channel_id=1, source_target_pairs={{0,12},{4,8},{8,4},{12,0},{1,13},{5,9},{9,5},{13,1},{2,14},{6,10},... | collective-permute-start | bytes 3145736 | tf_op jit(solution)/shard_map/ppermute | solution.py:233
  129.2 46.9 %collective-permute-start.9 = (bf16[16,128,256]{2,1,0:T(8,128)(2,1)}, bf16[16,128,256]{2,1,0:T(8,128)(2,1)}, u32[]{:S(2)}, u32[]{:S(2)}) collective-permute-start(bf16[16,128,256]{2,1,0:T(8,128)(2,1)} %get-tuple-element.53), channel_id=1, source_target_pairs={{0,4},{4,0},{8,12},{12,8},{1,5},{5,1},{9,13},{13,9},{2,6},{6,2},{1... | collective-permute-start | bytes 3145736 | tf_op jit(solution)/shard_map/ppermute | solution.py:233
  131.3 59.6 %copy-start.3 = (bf16[512,512]{1,0:T(8,128)(2,1)}, bf16[512,512]{1,0:T(8,128)(2,1)S(1)}, u32[]{:S(2)}) copy-start(bf16[512,512]{1,0:T(8,128)(2,1)S(1)} %pad_maximum_fusion.1.k_ref) | copy-start | bytes 1572868
  131.3 70.0 %collective-permute-start.10 = (bf16[16,128,256]{2,1,0:T(8,128)(2,1)S(1)}, bf16[16,128,256]{2,1,0:T(8,128)(2,1)}, u32[]{:S(2)}, u32[]{:S(2)}) collective-permute-start(bf16[16,128,256]{2,1,0:T(8,128)(2,1)S(1)} %get-tuple-element.42.refs_3_), channel_id=1, source_target_pairs={{0,8},{4,12},{8,0},{12,4},{1,9},{5,13},{9,1},{13,5},{2,10},{6,14},... | collective-permute-start | bytes 3145736 | tf_op jit(solution)/shard_map/ppermute | solution.py:233
  132.9 87.3 %collective-permute-start.11 = (bf16[16,128,256]{2,1,0:T(8,128)(2,1)}, bf16[16,128,256]{2,1,0:T(8,128)(2,1)}, u32[]{:S(2)}, u32[]{:S(2)}) collective-permute-start(bf16[16,128,256]{2,1,0:T(8,128)(2,1)} %copy-done.16), channel_id=1, source_target_pairs={{0,12},{4,8},{8,4},{12,0},{1,13},{5,9},{9,5},{13,1},{2,14},{6,10},... | collective-permute-start | bytes 3145736 | tf_op jit(solution)/shard_map/ppermute | solution.py:233
  153.8 89.8 %collective-permute-start.13 = (bf16[16,128,256]{2,1,0:T(8,128)(2,1)}, bf16[16,128,256]{2,1,0:T(8,128)(2,1)S(1)}, u32[]{:S(2)}, u32[]{:S(2)}) collective-permute-start(bf16[16,128,256]{2,1,0:T(8,128)(2,1)} %get-tuple-element.43.refs_9_), channel_id=1, source_target_pairs={{0,8},{4,12},{8,0},{12,4},{1,9},{5,13},{9,1},{13,5},{2,10},{6,14},... | collective-permute-start | bytes 3145736 | tf_op jit(solution)/shard_map/ppermute | solution.py:233
  175.2 54.2 %collective-permute-start.12 = (bf16[16,128,256]{2,1,0:T(8,128)(2,1)}, bf16[16,128,256]{2,1,0:T(8,128)(2,1)S(1)}, u32[]{:S(2)}, u32[]{:S(2)}) collective-permute-start(bf16[16,128,256]{2,1,0:T(8,128)(2,1)} %get-tuple-element.57), channel_id=1, source_target_pairs={{0,4},{4,0},{8,12},{12,8},{1,5},{5,1},{9,13},{13,9},{2,6},{6,2},{1... | collective-permute-start | bytes 3145736 | tf_op jit(solution)/shard_map/ppermute | solution.py:233
  176.1 88.3 %collective-permute-start.14 = (bf16[16,128,256]{2,1,0:T(8,128)(2,1)}, bf16[16,128,256]{2,1,0:T(8,128)(2,1)S(1)}, u32[]{:S(2)}, u32[]{:S(2)}) collective-permute-start(bf16[16,128,256]{2,1,0:T(8,128)(2,1)} %copy-done.13), channel_id=1, source_target_pairs={{0,12},{4,8},{8,4},{12,0},{1,13},{5,9},{9,5},{13,1},{2,14},{6,10},... | collective-permute-start | bytes 3145736 | tf_op jit(solution)/shard_map/ppermute | solution.py:233
  187.8 1.0 copy-start.11
  188.9 1.0 copy-start.12
  189.8 1.1 copy-start.15
  190.9 1.0 copy-start.4
  198.3 1.0 copy-start.7
  199.3 1.0 copy-start.10
  200.3 1.1 copy-start.17
  226.5 1.0 copy-start.5
  227.5 1.0 copy-start.6
  228.5 1.0 copy-start.14
  229.4 35.0 %copy-start.26 = (bf16[16,128,256]{2,1,0:T(8,128)(2,1)}, bf16[16,128,256]{2,1,0:T(8,128)(2,1)S(1)}, u32[]{:S(2)}) copy-start(bf16[16,128,256]{2,1,0:T(8,128)(2,1)S(1)} %collective-permute-done.12.refs_1_) | copy-start | bytes 3145732
  243.5 20.9 %copy-start.25 = (bf16[16,128,256]{2,1,0:T(8,128)(2,1)}, bf16[16,128,256]{2,1,0:T(8,128)(2,1)S(1)}, u32[]{:S(2)}) copy-start(bf16[16,128,256]{2,1,0:T(8,128)(2,1)S(1)} %collective-permute-done.13.refs_2_) | copy-start | bytes 3145732
  264.4 1.0 copy-start.27
  271.9 1.0 copy-start.2
  272.9 1.0 copy-start.8
  273.8 1.0 copy-start.9
  274.8 1.0 copy-start.19
  277.6 1.9 collective-permute-start.16
  280.4 8.8 %collective-permute-start.17 = (f32[256,256]{0,1:T(8,128)S(1)}, f32[256,256]{0,1:T(8,128)}, u32[]{:S(2)}, u32[]{:S(2)}) collective-permute-start(f32[256,256]{0,1:T(8,128)S(1)} %fusion.15), channel_id=1, source_target_pairs={{0,8},{4,12},{8,0},{12,4},{1,9},{5,13},{9,1},{13,5},{2,10},{6,14},... | collective-permute-start | bytes 786440 | tf_op jit(solution)/shard_map/ppermute | solution.py:233
  282.2 35.5 %collective-permute-start.21 = (bf16[16,128,256]{2,1,0:T(8,128)(2,1)}, bf16[16,128,256]{2,1,0:T(8,128)(2,1)}, u32[]{:S(2)}, u32[]{:S(2)}) collective-permute-start(bf16[16,128,256]{2,1,0:T(8,128)(2,1)} %copy-done.15), channel_id=1, source_target_pairs={{0,4},{4,0},{8,12},{12,8},{1,5},{5,1},{9,13},{13,9},{2,6},{6,2},{1... | collective-permute-start | bytes 3145736 | tf_op jit(solution)/shard_map/ppermute | solution.py:233
  282.3 36.7 %collective-permute-start.22 = (bf16[16,128,256]{2,1,0:T(8,128)(2,1)}, bf16[16,128,256]{2,1,0:T(8,128)(2,1)}, u32[]{:S(2)}, u32[]{:S(2)}) collective-permute-start(bf16[16,128,256]{2,1,0:T(8,128)(2,1)} %copy-done.17), channel_id=1, source_target_pairs={{0,4},{4,0},{8,12},{12,8},{1,5},{5,1},{9,13},{13,9},{2,6},{6,2},{1... | collective-permute-start | bytes 3145736 | tf_op jit(solution)/shard_map/ppermute | solution.py:233
  282.8 60.8 %collective-permute-start.23 = (bf16[16,128,256]{2,1,0:T(8,128)(2,1)}, bf16[16,128,256]{2,1,0:T(8,128)(2,1)}, u32[]{:S(2)}, u32[]{:S(2)}) collective-permute-start(bf16[16,128,256]{2,1,0:T(8,128)(2,1)} %copy-done.14), channel_id=1, source_target_pairs={{0,4},{4,0},{8,12},{12,8},{1,5},{5,1},{9,13},{13,9},{2,6},{6,2},{1... | collective-permute-start | bytes 3145736 | tf_op jit(solution)/shard_map/ppermute | solution.py:233
  282.8 62.2 %collective-permute-start.24 = (bf16[16,128,256]{2,1,0:T(8,128)(2,1)}, bf16[16,128,256]{2,1,0:T(8,128)(2,1)}, u32[]{:S(2)}, u32[]{:S(2)}) collective-permute-start(bf16[16,128,256]{2,1,0:T(8,128)(2,1)} %copy-done.19), channel_id=1, source_target_pairs={{0,4},{4,0},{8,12},{12,8},{1,5},{5,1},{9,13},{13,9},{2,6},{6,2},{1... | collective-permute-start | bytes 3145736 | tf_op jit(solution)/shard_map/ppermute | solution.py:233
  289.2 57.4 %collective-permute-start.25 = (bf16[16,128,256]{2,1,0:T(8,128)(2,1)}, bf16[16,128,256]{2,1,0:T(8,128)(2,1)}, u32[]{:S(2)}, u32[]{:S(2)}) collective-permute-start(bf16[16,128,256]{2,1,0:T(8,128)(2,1)} %copy-done.12), channel_id=1, source_target_pairs={{0,8},{4,12},{8,0},{12,4},{1,9},{5,13},{9,1},{13,5},{2,10},{6,14},... | collective-permute-start | bytes 3145736 | tf_op jit(solution)/shard_map/ppermute | solution.py:233
  291.7 0.7 copy-start.23
  317.7 28.9 %collective-permute-start.26 = (bf16[16,128,256]{2,1,0:T(8,128)(2,1)}, bf16[16,128,256]{2,1,0:T(8,128)(2,1)}, u32[]{:S(2)}, u32[]{:S(2)}) collective-permute-start(bf16[16,128,256]{2,1,0:T(8,128)(2,1)} %copy-done.11), channel_id=1, source_target_pairs={{0,12},{4,8},{8,4},{12,0},{1,13},{5,9},{9,5},{13,1},{2,14},{6,10},... | collective-permute-start | bytes 3145736 | tf_op jit(solution)/shard_map/ppermute | solution.py:233
  319.0 45.8 %collective-permute-start.27 = (bf16[16,128,256]{2,1,0:T(8,128)(2,1)}, bf16[16,128,256]{2,1,0:T(8,128)(2,1)}, u32[]{:S(2)}, u32[]{:S(2)}) collective-permute-start(bf16[16,128,256]{2,1,0:T(8,128)(2,1)} %copy-done.10), channel_id=1, source_target_pairs={{0,8},{4,12},{8,0},{12,4},{1,9},{5,13},{9,1},{13,5},{2,10},{6,14},... | collective-permute-start | bytes 3145736 | tf_op jit(solution)/shard_map/ppermute | solution.py:233
  343.6 44.9 %collective-permute-start.28 = (bf16[16,128,256]{2,1,0:T(8,128)(2,1)}, bf16[16,128,256]{2,1,0:T(8,128)(2,1)}, u32[]{:S(2)}, u32[]{:S(2)}) collective-permute-start(bf16[16,128,256]{2,1,0:T(8,128)(2,1)} %copy-done.7), channel_id=1, source_target_pairs={{0,12},{4,8},{8,4},{12,0},{1,13},{5,9},{9,5},{13,1},{2,14},{6,10},... | collective-permute-start | bytes 3145736 | tf_op jit(solution)/shard_map/ppermute | solution.py:233
  345.1 138.3 %collective-permute-start.18 = (bf16[16,128,256]{2,1,0:T(8,128)(2,1)}, bf16[16,128,256]{2,1,0:T(8,128)(2,1)}, u32[]{:S(2)}, u32[]{:S(2)}) collective-permute-start(bf16[16,128,256]{2,1,0:T(8,128)(2,1)} %copy-done.9), channel_id=1, source_target_pairs={{0,8},{4,12},{8,0},{12,4},{1,9},{5,13},{9,1},{13,5},{2,10},{6,14},... | collective-permute-start | bytes 3145736 | tf_op jit(solution)/shard_map/ppermute | solution.py:233
  346.6 130.3 %collective-permute-start.19 = (bf16[16,128,256]{2,1,0:T(8,128)(2,1)}, bf16[16,128,256]{2,1,0:T(8,128)(2,1)}, u32[]{:S(2)}, u32[]{:S(2)}) collective-permute-start(bf16[16,128,256]{2,1,0:T(8,128)(2,1)} %copy-done.5), channel_id=1, source_target_pairs={{0,12},{4,8},{8,4},{12,0},{1,13},{5,9},{9,5},{13,1},{2,14},{6,10},... | collective-permute-start | bytes 3145736 | tf_op jit(solution)/shard_map/ppermute | solution.py:233
  346.6 123.7 %collective-permute-start.20 = (bf16[16,128,256]{2,1,0:T(8,128)(2,1)}, bf16[16,128,256]{2,1,0:T(8,128)(2,1)}, u32[]{:S(2)}, u32[]{:S(2)}) collective-permute-start(bf16[16,128,256]{2,1,0:T(8,128)(2,1)} %copy-done.6), channel_id=1, source_target_pairs={{0,8},{4,12},{8,0},{12,4},{1,9},{5,13},{9,1},{13,5},{2,10},{6,14},... | collective-permute-start | bytes 3145736 | tf_op jit(solution)/shard_map/ppermute | solution.py:233
  364.8 125.0 %collective-permute-start.15 = (bf16[16,128,256]{2,1,0:T(8,128)(2,1)}, bf16[16,128,256]{2,1,0:T(8,128)(2,1)S(1)}, u32[]{:S(2)}, u32[]{:S(2)}) collective-permute-start(bf16[16,128,256]{2,1,0:T(8,128)(2,1)} %copy-done.8), channel_id=1, source_target_pairs={{0,12},{4,8},{8,4},{12,0},{1,13},{5,9},{9,5},{13,1},{2,14},{6,10},... | collective-permute-start | bytes 3145736 | tf_op jit(solution)/shard_map/ppermute | solution.py:233
where the time goes:
time: 497 us; the launch traced here: 495 us
  Pallas kernels  198 us (40%)
  waiting for transfers between devices  182 us (37%)
  other arithmetic  52.3 us (11%)
  local copies, waits for them, and re-layouts  33.4 us (7%)
  starting transfers between devices  24.3 us (5%)
    ppermute x29, waiting for transfers between devices, swap(): return lax.ppermute(value, 'site', [(s, s ^ d) for s in range(count)])  182 us
    pallas_call x5, Pallas kernels, orthonormal_rows(): pl.pallas_call(functools.partial(out_body, parts, steps, lines, sites), g...  107 us
    pallas_call x5, Pallas kernels, apply_y(): pl.pallas_call(functools.partial(y_body, parts, rows, TILE), grid_spec=pl...  65.3 us
    pallas_call x4, Pallas kernels, apply_x(): pl.pallas_call(functools.partial(x_body, count, lines, own), grid=(rows /...  25.5 us
    ppermute x29, starting transfers between devices, swap(): return lax.ppermute(value, 'site', [(s, s ^ d) for s in range(count)])  24.3 us
    unnamed x57, local copies, waits for them, and re-layouts  22.8 us
    another operation x4, other arithmetic, small_inverse(): return jax.scipy.linalg.solve_triangular(lower, identity, lower=True)  21.8 us
    another operation x3, other arithmetic, factorize(): first = jnp.linalg.cholesky(gram[:half, :half])  12.5 us
  transfers between devices with their start and end apart: 29, of which 12 were waited for; matrix products, arithmetic and copies ran while one was open for 13% of the time, Pallas kernels for 24%

commit v1 on v0

--- a/solution.py
+++ b/solution.py
@@ -8,40 +8,38 @@
 from jax.sharding import PartitionSpec as P
 
 CORES = 2
-LANES = 128
 TILE = 16
 CHUNKS = 4
-UNROLL = 8
 LINES = 4
 VMEM = 48 * 1024 * 1024
 
 
-def put(acc, row, value):
-    for lane in range(acc.shape[0]):
-        acc[lane, row : row + value.shape[0], :] = value[:, lane * LANES : (lane + 1) * LANES]
-
-
-def take(acc, row, count, stride, out, place):
-    for lane in range(acc.shape[0]):
-        out[place, :, lane * LANES : (lane + 1) * LANES] = acc[
-            lane, pl.ds(row, count, stride=stride), :
-        ].astype(jnp.bfloat16)
+def make_swap(perm):
+    @pl.when(pl.program_id(0) == 0)
+    def _():
+        to = lax.broadcasted_iota(jnp.int32, perm.shape, 0)
+        source = lax.broadcasted_iota(jnp.int32, perm.shape, 1)
+        hit = (to % TILE == source // TILE) & (to // TILE == source % TILE)
+        perm[...] = jnp.where(hit, 1.0, 0.0).astype(jnp.bfloat16)
+
+
+def swapped(perm, value):
+    return jnp.dot(perm[...], value, preferred_element_type=jnp.float32).astype(jnp.bfloat16)
 
 
 def y_body(parts, rows, sites, base_ref, *refs):
-    kinetic, w_ref, outs, acc = refs[:parts], refs[parts], refs[-parts - 1 : -1], refs[-1]
-    every = parts * rows
+    kinetic, w_ref, outs = refs[:parts], refs[parts], refs[-parts - 2 : -2]
+    acc, perm = refs[-2:]
+    make_swap(perm)
     left = jnp.concatenate([k[...] for k in kinetic], axis=0)
-
     for x in range(sites):
-        put(acc, x * every, jnp.dot(left, w_ref[x], preferred_element_type=jnp.float32))
-
+        value = jnp.dot(left, w_ref[x], preferred_element_type=jnp.float32)
+        acc[:, x] = value.astype(jnp.bfloat16).reshape(-1, TILE, value.shape[1])
     for part in range(parts):
-
-        @pl.loop(0, rows, step=UNROLL)
-        def _(first, part=part):
-            for y in range(UNROLL):
-                take(acc, part * rows + first + y, sites, every, outs[part], first + y)
+        for first in range(0, rows, TILE):
+            group = acc[(part * rows + first) // TILE]
+            done = swapped(perm, group.reshape(-1, group.shape[-1]))
+            outs[part][first : first + TILE] = done.reshape(group.shape)
 
 
 def apply_y(walker, kinetic, bases, rows, after):
@@ -61,7 +59,10 @@
             grid=(own // TILE,),
             in_specs=specs,
             out_specs=[pl.BlockSpec((rows, TILE, orbitals), lambda i, b: (0, i, 0))] * parts,
-            scratch_shapes=[pltpu.VMEM((orbitals // LANES, TILE * every, LANES), jnp.float32)],
+            scratch_shapes=[
+                pltpu.VMEM((every // TILE, TILE, TILE, orbitals), jnp.bfloat16),
+                pltpu.VMEM((TILE * TILE, TILE * TILE), jnp.bfloat16),
+            ],
         ),
         out_shape=[jax.ShapeDtypeStruct((rows, own, orbitals), jnp.bfloat16)] * parts,
         compiler_params=pltpu.CompilerParams(vmem_limit_bytes=VMEM),
@@ -122,32 +123,26 @@
     return outs[:count], outs[count]
 
 
-def out_body(parts, steps, lines, sites, base_ref, *refs):
-    ins, v_ref, out, held, acc = refs[:parts], refs[parts], refs[-3], refs[-2], refs[-1]
+def out_body(parts, steps, sites, base_ref, *refs):
+    ins, v_ref, out, held, perm = refs[:parts], refs[parts], refs[-3], refs[-2], refs[-1]
+    make_swap(perm)
     for p in range(parts):
 
         @pl.when(pl.program_id(0) // steps == p)
         def _(p=p):
             held[...] = ins[p][...]
 
-    @pl.loop(0, lines, step=4)
-    def _(first):
-        for y in range(4):
-            row = pl.multiple_of((first + y) * sites, sites)
-            value = jnp.dot(held[first + y], v_ref[...], preferred_element_type=jnp.float32)
-            for lane in range(acc.shape[0]):
-                acc[lane, pl.ds(row, sites), :] = value[:, lane * LANES : (lane + 1) * LANES]
-
-    @pl.loop(0, sites, step=UNROLL)
-    def _(first):
-        for x in range(UNROLL):
-            take(acc, first + x, lines, sites, out, first + x)
+    for first in range(0, sites, TILE):
+        group = held[:, first : first + TILE, :]
+        rows = swapped(perm, group.reshape(-1, group.shape[-1]))
+        value = jnp.dot(rows, v_ref[...], preferred_element_type=jnp.float32)
+        out[first : first + TILE] = value.astype(jnp.bfloat16).reshape(group.shape)
 
 
 def orthonormal_rows(pieces, inverse, bases, result, shape):
     parts = len(pieces)
     rows, own, orbitals = pieces[0].shape
-    lines, sites = TILE, min(own, 32)
+    lines, sites = TILE, min(own, 64)
     across = own // sites
     steps = (rows // lines) * across
 
@@ -171,7 +166,7 @@
         operands.append(result)
         aliases = {parts + 2: 0}
     return pl.pallas_call(
-        functools.partial(out_body, parts, steps, lines, sites),
+        functools.partial(out_body, parts, steps, sites),
         grid_spec=pltpu.PrefetchScalarGridSpec(
             num_scalar_prefetch=1,
             grid=(parts * steps,),
@@ -179,7 +174,7 @@
             out_specs=pl.BlockSpec((sites, lines, orbitals), out_at),
             scratch_shapes=[
                 pltpu.VMEM((lines, sites, orbitals), jnp.bfloat16),
-                pltpu.VMEM((orbitals // LANES, lines * sites, LANES), jnp.float32),
+                pltpu.VMEM((TILE * TILE, TILE * TILE), jnp.bfloat16),
             ],
         ),
         out_shape=jax.ShapeDtypeStruct(shape, jnp.bfloat16),

time: 497 us -> 474 us (0.954)
  Pallas kernels: 198 us -> 125 us
  waiting for transfers between devices: 182 us -> 233 us
    pallas_call x5, Pallas kernels: 107 us -> 40.9 us  [orthonormal_rows(): pl.pallas_call(functools.partial(out_body, parts, steps, sites), grid_spe...]
    ppermute x29, waiting for transfers between devices: 182 us -> 233 us  [swap(): return lax.ppermute(value, 'site', [(s, s ^ d) for s in range(count)])]
    pallas_call x5, Pallas kernels: 65.3 us -> 58.3 us  [apply_y(): pl.pallas_call(functools.partial(y_body, parts, rows, TILE), grid_spec=pl...]
  transfers between devices with their start and end apart: 29 -> 29, of which waited for: 12 -> 14; matrix products, arithmetic and copies ran while one was open for 13% -> 14% of each run, Pallas kernels for 24% -> 12%
where the time goes in v1:
time: 474 us; the launch traced here: 473 us
  waiting for transfers between devices  233 us (49%)
  Pallas kernels  125 us (26%)
  other arithmetic  52.3 us (11%)
  local copies, waits for them, and re-layouts  33.4 us (7%)
  starting transfers between devices  24.3 us (5%)
    ppermute x29, waiting for transfers between devices, swap(): return lax.ppermute(value, 'site', [(s, s ^ d) for s in range(count)])  233 us
    pallas_call x5, Pallas kernels, apply_y(): pl.pallas_call(functools.partial(y_body, parts, rows, TILE), grid_spec=pl...  58.3 us
    pallas_call x5, Pallas kernels, orthonormal_rows(): pl.pallas_call(functools.partial(out_body, parts, steps, sites), grid_spe...  40.9 us
    pallas_call x4, Pallas kernels, apply_x(): pl.pallas_call(functools.partial(x_body, count, lines, own), grid=(rows /...  25.5 us
    ppermute x29, starting transfers between devices, swap(): return lax.ppermute(value, 'site', [(s, s ^ d) for s in range(count)])  24.3 us
    unnamed x57, local copies, waits for them, and re-layouts  22.8 us
    another operation x4, other arithmetic, small_inverse(): return jax.scipy.linalg.solve_triangular(lower, identity, lower=True)  21.8 us
    another operation x3, other arithmetic, factorize(): first = jnp.linalg.cholesky(gram[:half, :half])  12.5 us
  transfers between devices with their start and end apart: 29, of which 14 were waited for; matrix products, arithmetic and copies ran while one was open for 14% of the time, Pallas kernels for 12%

profile of v1, /device:TPU:0, one launch (start us, length us, event | category | flops | bytes accessed | tf_op | source)
XLA Modules:
  0.0 472.9 jit_solution(15139930453909771942)
XLA Ops:
  1.7 11.6 %apply_y.5 = (bf16[16,128,256]{2,1,0:T(8,128)(2,1)S(1)}, bf16[16,128,256]{2,1,0:T(8,128)(2,1)}) custom-call(s32[2]{0:T(128)S(1)} %get-tuple-element.96.base_ref, bf16[256,256]{1,0:T(8,128)(2,1)S(1)} %copy-done, bf16[256,256]{1,0:T(8,128)(2,1)S(1)} %copy-done, bf16[128,256,256]{2,1,0:T(8,128)(2,1)} %bitcast.59), custom_call_target="tpu_custom_call" | custom-call | flops 536870912 | bytes 18874368 | tf_op jit(solution)/shard_map/apply_y/pallas_call | solution.py:55
  13.4 10.9 %apply_y.6 = (bf16[16,128,256]{2,1,0:T(8,128)(2,1)S(1)}, bf16[16,128,256]{2,1,0:T(8,128)(2,1)S(1)}) custom-call(s32[2]{0:T(128)S(1)} %get-tuple-element.97.base_ref, bf16[256,256]{1,0:T(8,128)(2,1)S(1)} %copy-done.1, bf16[256,256]{1,0:T(8,128)(2,1)S(1)} %copy-done.1, bf16[128,256,256]{2,1,0:T(8,128)(2,1)} %bitcast.60, ...), custom_call_target="tpu_custom_call" | custom-call | flops 536870912 | bytes 18874368 | tf_op jit(solution)/shard_map/apply_y/pallas_call | solution.py:55
  24.3 1.0 copy-done.22
  25.4 10.9 %apply_y.7 = (bf16[16,128,256]{2,1,0:T(8,128)(2,1)S(1)}, bf16[16,128,256]{2,1,0:T(8,128)(2,1)S(1)}) custom-call(s32[2]{0:T(128)S(1)} %get-tuple-element.98.base_ref, bf16[256,256]{1,0:T(8,128)(2,1)S(1)} %copy-done.1, bf16[256,256]{1,0:T(8,128)(2,1)S(1)} %copy-done.1, bf16[128,256,256]{2,1,0:T(8,128)(2,1)} %bitcast.61, ...), custom_call_target="tpu_custom_call" | custom-call | flops 536870912 | bytes 18874368 | tf_op jit(solution)/shard_map/apply_y/pallas_call | solution.py:55
  36.3 1.0 copy-done.16
  37.3 11.6 %apply_y.8 = (bf16[16,128,256]{2,1,0:T(8,128)(2,1)}, bf16[16,128,256]{2,1,0:T(8,128)(2,1)S(1)}) custom-call(s32[2]{0:T(128)S(1)} %get-tuple-element.99.base_ref, bf16[256,256]{1,0:T(8,128)(2,1)S(1)} %copy-done.1, bf16[256,256]{1,0:T(8,128)(2,1)S(1)} %copy-done.1, bf16[128,256,256]{2,1,0:T(8,128)(2,1)} %bitcast.62, ...), custom_call_target="tpu_custom_call" | custom-call | flops 536870912 | bytes 18874368 | tf_op jit(solution)/shard_map/apply_y/pallas_call | solution.py:55
  49.9 13.3 %apply_y.9 = (bf16[16,128,256]{2,1,0:T(8,128)(2,1)S(1)}, bf16[16,128,256]{2,1,0:T(8,128)(2,1)}, bf16[16,128,256]{2,1,0:T(8,128)(2,1)S(1)}, bf16[16,128,256]{2,1,...) custom-call(s32[8]{0:T(128)S(1)} %and_select_fusion.5.base_ref, ...), custom_call_target="tpu_custom_call" | custom-call | flops 2147483648 | bytes 25165824 | tf_op jit(solution)/shard_map/apply_y/pallas_call | solution.py:55
  63.2 1.0 copy-done.18
  64.2 1.1 copy-done.20
  65.3 1.1 copy-done.21
  66.8 2.5 collective-permute-start.4
  69.7 1.8 collective-permute-start.2
  71.6 44.1 %collective-permute-done.2 = bf16[128,64]{0,1:T(8,128)(2,1)S(1)} collective-permute-done((bf16[128,64]{0,1:T(8,128)(2,1)S(1)}, bf16[128,64]{0,1:T(8,128)(2,1)S(1)}, u32[]{:S(2)}, u32[]{:S(2)}) %collective-permute-start.2) | collective-permute-done | bytes 16416 | tf_op jit(solution)/shard_map/ppermute | solution.py:228
  115.8 1.5 collective-permute-start.1
  117.3 2.2 collective-permute-done.1
  119.5 1.2 collective-permute-done
  120.7 1.5 collective-permute-start.7
  123.0 1.1 constant_dynamic-slice_fusion.11
  124.4 1.5 collective-permute-start.10
  126.0 2.7 copy.40
  128.6 18.2 %collective-permute-done.7.refs_2_ = bf16[16,128,256]{2,1,0:T(8,128)(2,1)} collective-permute-done((bf16[16,128,256]{2,1,0:T(8,128)(2,1)S(1)}, bf16[16,128,256]{2,1,0:T(8,128)(2,1)}, u32[]{:S(2)}, u32[]{:S(2)}) %collective-permute-start.7) | collective-permute-done | bytes 1048608 | tf_op jit(solution)/shard_map/ppermute | solution.py:228
  146.8 1.5 collective-permute-start.13
  148.3 20.0 %collective-permute-done.8.refs_3_ = bf16[16,128,256]{2,1,0:T(8,128)(2,1)} collective-permute-done((bf16[16,128,256]{2,1,0:T(8,128)(2,1)}, bf16[16,128,256]{2,1,0:T(8,128)(2,1)}, u32[]{:S(2)}, u32[]{:S(2)}) %collective-permute-start.8) | collective-permute-done | bytes 1048608 | tf_op jit(solution)/shard_map/ppermute | solution.py:228
  169.1 1.1 collective-permute-start.14
  170.2 4.3 fusion.17
  174.5 6.3 %apply_x.4 = (bf16[16,128,256]{2,1,0:T(8,128)(2,1)S(1)}, bf16[16,128,256]{2,1,0:T(8,128)(2,1)S(1)}, bf16[16,128,256]{2,1,0:T(8,128)(2,1)S(1)}, bf16[16,128,256]{2,1,0:T(8,128)(2,1)S(1)}, f32[256,256]{1,0:T(8,128)S(1)}) custom-call(bf16[512,512]{1,0:T(8,128)(2,1)S(1)} %pad_maximum_fusion.1.k_ref, f32[4,512,4]{2,1,0:T(8,128)} %get-tuple-element.80.f_ref, ...), custom_call_target="tpu_custom_call" | custom-call | flops 3221225472 | bytes 8388608 | tf_op jit(solution)/shard_map/apply_x/pallas_call | solution.py:103
  180.9 1.0 copy-done.11
  182.9 1.1 copy-done.15
  184.0 1.0 copy-done.4
  185.0 6.3 %apply_x.5 = (bf16[16,128,256]{2,1,0:T(8,128)(2,1)S(1)}, bf16[16,128,256]{2,1,0:T(8,128)(2,1)S(1)}, bf16[16,128,256]{2,1,0:T(8,128)(2,1)S(1)}, bf16[16,128,256]{2,1,0:T(8,128)(2,1)S(1)}, f32[256,256]{1,0:T(8,128)S(1)}) custom-call(bf16[512,512]{1,0:T(8,128)(2,1)S(1)} %copy-done.4, f32[4,512,4]{2,1,0:T(8,128)} %get-tuple-element.81.f_ref, ...), custom_call_target="tpu_custom_call" | custom-call | flops 3221225472 | bytes 8388608 | tf_op jit(solution)/shard_map/apply_x/pallas_call | solution.py:103
  191.3 1.0 copy-done.7
  192.3 1.0 copy-done.10
  193.3 1.1 copy-done.17
  194.4 18.8 %collective-permute-done.11.refs_3_ = bf16[16,128,256]{2,1,0:T(8,128)(2,1)} collective-permute-done((bf16[16,128,256]{2,1,0:T(8,128)(2,1)}, bf16[16,128,256]{2,1,0:T(8,128)(2,1)}, u32[]{:S(2)}, u32[]{:S(2)}) %collective-permute-start.11) | collective-permute-done | bytes 1048608 | tf_op jit(solution)/shard_map/ppermute | solution.py:228
  213.2 6.3 %apply_x.6 = (bf16[16,128,256]{2,1,0:T(8,128)(2,1)S(1)}, bf16[16,128,256]{2,1,0:T(8,128)(2,1)S(1)}, bf16[16,128,256]{2,1,0:T(8,128)(2,1)S(1)}, bf16[16,128,256]{2,1,0:T(8,128)(2,1)S(1)}, f32[256,256]{1,0:T(8,128)S(1)}) custom-call(bf16[512,512]{1,0:T(8,128)(2,1)S(1)} %copy-done.4, f32[4,512,4]{2,1,0:T(8,128)} %get-tuple-element.82.f_ref, ...), custom_call_target="tpu_custom_call" | custom-call | flops 3221225472 | bytes 8388608 | tf_op jit(solution)/shard_map/apply_x/pallas_call | solution.py:103
  220.5 1.0 copy-done.6
  222.5 14.1 %collective-permute-done.13.refs_2_ = bf16[16,128,256]{2,1,0:T(8,128)(2,1)S(1)} collective-permute-done((bf16[16,128,256]{2,1,0:T(8,128)(2,1)}, bf16[16,128,256]{2,1,0:T(8,128)(2,1)S(1)}, u32[]{:S(2)}, u32[]{:S(2)}) %collective-permute-start.13) | collective-permute-done | bytes 1048608 | tf_op jit(solution)/shard_map/ppermute | solution.py:228
  236.6 20.9 %collective-permute-done.14.refs_3_ = bf16[16,128,256]{2,1,0:T(8,128)(2,1)S(1)} collective-permute-done((bf16[16,128,256]{2,1,0:T(8,128)(2,1)}, bf16[16,128,256]{2,1,0:T(8,128)(2,1)S(1)}, u32[]{:S(2)}, u32[]{:S(2)}) %collective-permute-start.14) | collective-permute-done | bytes 1048608 | tf_op jit(solution)/shard_map/ppermute | solution.py:228
  258.4 6.5 %apply_x.7 = (bf16[16,128,256]{2,1,0:T(8,128)(2,1)S(1)}, bf16[16,128,256]{2,1,0:T(8,128)(2,1)S(1)}, bf16[16,128,256]{2,1,0:T(8,128)(2,1)S(1)}, bf16[16,128,256]{2,1,0:T(8,128)(2,1)S(1)}, f32[256,256]{1,0:T(8,128)S(1)}) custom-call(bf16[512,512]{1,0:T(8,128)(2,1)S(1)} %copy-done.4, f32[4,512,4]{2,1,0:T(8,128)} %get-tuple-element.83.f_ref, ...), custom_call_target="tpu_custom_call" | custom-call | flops 3221225472 | bytes 8388608 | tf_op jit(solution)/shard_map/apply_x/pallas_call | solution.py:103
  271.3 1.2 collective-permute-done.16
  272.5 1.0 fusion.15
  273.5 1.5 collective-permute-start.17
  276.3 5.9 %collective-permute-done.17 = f32[256,256]{0,1:T(8,128)} collective-permute-done((f32[256,256]{0,1:T(8,128)S(1)}, f32[256,256]{0,1:T(8,128)}, u32[]{:S(2)}, u32[]{:S(2)}) %collective-permute-start.17) | collective-permute-done | bytes 262176 | tf_op jit(solution)/shard_map/ppermute | solution.py:228
  282.3 1.5 collective-permute-start.25
  283.7 1.0 add.126
  286.4 11.7 %cholesky.44 = f32[128,128]{1,0:T(8,128)S(1)} custom-call(f32[128,128]{1,0:T(8,128)S(1)} %fusion.13), custom_call_target="Cholesky" | custom-call | tf_op jit(solution)/shard_map/jit(cholesky)/cholesky | solution.py:204
  299.6 9.8 %custom-call.6 = f32[1,128,128]{1,2,0:T(8,128)S(1)} custom-call(f32[1,128,128]{2,1,0:T(8,128)S(1)} %get-tuple-element.78), custom_call_target="InvertDiagBlocksLowerTriangular" | custom-call | tf_op jit(solution)/shard_map/jit(_solve_triangular)/triangular_solve | solution.py:198
  309.7 1.0 fusion.8
  310.8 1.1 slice_subtract_fusion
  313.0 11.7 %cholesky.55 = f32[128,128]{1,0:T(8,128)S(1)} custom-call(f32[128,128]{1,0:T(8,128)S(1)} %fusion.11), custom_call_target="Cholesky" | custom-call | tf_op jit(solution)/shard_map/jit(cholesky)/cholesky | solution.py:207
  326.0 10.6 %custom-call.7 = f32[1,128,128]{1,2,0:T(8,128)} custom-call(f32[1,128,128]{2,1,0:T(8,128)S(1)} %get-tuple-element.76), custom_call_target="InvertDiagBlocksLowerTriangular" | custom-call | tf_op jit(solution)/shard_map/jit(_solve_triangular)/triangular_solve | solution.py:198
  336.6 1.2 collective-permute-start.28
  338.1 1.5 collective-permute-start.18
  340.5 1.1 fusion.4
  342.4 15.4 %collective-permute-done.27.refs_10_ = bf16[16,128,256]{2,1,0:T(8,128)(2,1)} collective-permute-done((bf16[16,128,256]{2,1,0:T(8,128)(2,1)}, bf16[16,128,256]{2,1,0:T(8,128)(2,1)}, u32[]{:S(2)}, u32[]{:S(2)}) %collective-permute-start.27) | collective-permute-done | bytes 1048608 | tf_op jit(solution)/shard_map/ppermute | solution.py:228
  357.9 1.4 collective-permute-start.15
  361.1 20.4 %collective-permute-done.28.refs_11_ = bf16[16,128,256]{2,1,0:T(8,128)(2,1)} collective-permute-done((bf16[16,128,256]{2,1,0:T(8,128)(2,1)}, bf16[16,128,256]{2,1,0:T(8,128)(2,1)}, u32[]{:S(2)}, u32[]{:S(2)}) %collective-permute-start.28) | collective-permute-done | bytes 1048608 | tf_op jit(solution)/shard_map/ppermute | solution.py:228
  381.5 29.4 %orthonormal_rows.5.refs_2_ = bf16[128,256,256]{2,1,0:T(8,128)(2,1)} custom-call(s32[12]{0:T(128)S(1)} %and_select_fusion.base_ref, bf16[16,128,256]{2,1,0:T(8,128)(2,1)S(1)} %get-tuple-element.64.refs_0_, bf16[16,128,256]{2,1,0:T(8,128)(2,1)} %collective-permute-done.21.refs_1_, bf16[16,128,256]{2,1,0:T(8,128)(2,1)S(1)} %get-tuple-element.66.refs_2_, ...), custom_call_target="tpu_custom_call" | custom-call | flops 3221225472 | bytes 25165824 | tf_op jit(solution)/shard_map/orthonormal_rows/pallas_call | solution.py:168
  410.9 36.9 %collective-permute-done.20.refs_0_ = bf16[16,128,256]{2,1,0:T(8,128)(2,1)} collective-permute-done((bf16[16,128,256]{2,1,0:T(8,128)(2,1)}, bf16[16,128,256]{2,1,0:T(8,128)(2,1)}, u32[]{:S(2)}, u32[]{:S(2)}) %collective-permute-start.20) | collective-permute-done | bytes 1048608 | tf_op jit(solution)/shard_map/ppermute | solution.py:228
  447.7 3.1 orthonormal_rows.6.refs_2_
  450.9 3.1 orthonormal_rows.7.refs_2_
  454.0 3.1 orthonormal_rows.8.refs_2_
  457.1 13.6 %collective-permute-done.15.refs_0_ = bf16[16,128,256]{2,1,0:T(8,128)(2,1)S(1)} collective-permute-done((bf16[16,128,256]{2,1,0:T(8,128)(2,1)}, bf16[16,128,256]{2,1,0:T(8,128)(2,1)S(1)}, u32[]{:S(2)}, u32[]{:S(2)}) %collective-permute-start.15) | collective-permute-done | bytes 1048608 | tf_op jit(solution)/shard_map/ppermute | solution.py:228
  470.7 2.2 orthonormal_rows.9
  (117 shorter events, 26.2 us)
Async XLA Ops:
  0.8 0.9 copy-start
  1.7 11.6 %copy-start.1 = (bf16[256,256]{1,0:T(8,128)(2,1)S(1)}, bf16[256,256]{1,0:T(8,128)(2,1)}, u32[]{:S(2)}) copy-start(bf16[256,256]{1,0:T(8,128)(2,1)} %refs_7_.1) | copy-start | bytes 393220
  24.3 1.0 copy-start.22
  36.3 1.0 copy-start.16
  37.3 32.3 %copy-start.24 = (bf16[1,1,128,256]{3,2,1,0:T(8,128)(2,1)S(1)}, bf16[1,1,128,256]{3,2,1,0:T(8,128)(2,1)}, u32[]{:S(2)}) copy-start(bf16[1,1,128,256]{3,2,1,0:T(8,128)(2,1)} %param.8) | copy-start | bytes 196612
  48.9 1.0 copy-start.13
  63.2 1.0 copy-start.18
  64.2 1.1 copy-start.20
  65.3 1.1 copy-start.21
  66.3 55.8 %collective-permute-start.3 = (bf16[16,128,256]{2,1,0:T(8,128)(2,1)}, bf16[16,128,256]{2,1,0:T(8,128)(2,1)}, u32[]{:S(2)}, u32[]{:S(2)}) collective-permute-start(bf16[16,128,256]{2,1,0:T(8,128)(2,1)} %get-tuple-element.45), channel_id=1, source_target_pairs={{0,4},{4,0},{8,12},{12,8},{1,5},{5,1},{9,13},{13,9},{2,6},{6,2},{1... | collective-permute-start | bytes 3145736 | tf_op jit(solution)/shard_map/ppermute | solution.py:228
  66.8 55.4 %collective-permute-start.4 = (bf16[16,128,256]{2,1,0:T(8,128)(2,1)S(1)}, bf16[16,128,256]{2,1,0:T(8,128)(2,1)}, u32[]{:S(2)}, u32[]{:S(2)}) collective-permute-start(bf16[16,128,256]{2,1,0:T(8,128)(2,1)S(1)} %get-tuple-element.40.refs_3_), channel_id=1, source_target_pairs={{0,8},{4,12},{8,0},{12,4},{1,9},{5,13},{9,1},{13,5},{2,10},{6,14},... | collective-permute-start | bytes 3145736 | tf_op jit(solution)/shard_map/ppermute | solution.py:228
  69.3 55.1 %collective-permute-start.5 = (bf16[16,128,256]{2,1,0:T(8,128)(2,1)}, bf16[16,128,256]{2,1,0:T(8,128)(2,1)}, u32[]{:S(2)}, u32[]{:S(2)}) collective-permute-start(bf16[16,128,256]{2,1,0:T(8,128)(2,1)} %get-tuple-element.46), channel_id=1, source_target_pairs={{0,12},{4,8},{8,4},{12,0},{1,13},{5,9},{9,5},{13,1},{2,14},{6,10},... | collective-permute-start | bytes 3145736 | tf_op jit(solution)/shard_map/ppermute | solution.py:228
  69.4 56.5 %collective-permute-start.6 = (bf16[16,128,256]{2,1,0:T(8,128)(2,1)}, bf16[16,128,256]{2,1,0:T(8,128)(2,1)}, u32[]{:S(2)}, u32[]{:S(2)}) collective-permute-start(bf16[16,128,256]{2,1,0:T(8,128)(2,1)} %get-tuple-element.49), channel_id=1, source_target_pairs={{0,4},{4,0},{8,12},{12,8},{1,5},{5,1},{9,13},{13,9},{2,6},{6,2},{1... | collective-permute-start | bytes 3145736 | tf_op jit(solution)/shard_map/ppermute | solution.py:228
  69.7 46.0 %collective-permute-start.2 = (bf16[128,64]{0,1:T(8,128)(2,1)S(1)}, bf16[128,64]{0,1:T(8,128)(2,1)S(1)}, u32[]{:S(2)}, u32[]{:S(2)}) collective-permute-start(bf16[128,64]{0,1:T(8,128)(2,1)S(1)} %bitcast.69), channel_id=1, source_target_pairs={{0,12},{4,8},{8,4},{12,0},{1,13},{5,9},{9,5},{13,1},{2,14},{6,10},... | collective-permute-start | bytes 49160 | tf_op jit(solution)/shard_map/ppermute | solution.py:228
  115.8 3.7 collective-permute-start.1
  119.5 1.2 collective-permute-start
  120.7 26.1 %collective-permute-start.7 = (bf16[16,128,256]{2,1,0:T(8,128)(2,1)S(1)}, bf16[16,128,256]{2,1,0:T(8,128)(2,1)}, u32[]{:S(2)}, u32[]{:S(2)}) collective-permute-start(bf16[16,128,256]{2,1,0:T(8,128)(2,1)S(1)} %get-tuple-element.41.refs_3_), channel_id=1, source_target_pairs={{0,8},{4,12},{8,0},{12,4},{1,9},{5,13},{9,1},{13,5},{2,10},{6,14},... | collective-permute-start | bytes 3145736 | tf_op jit(solution)/shard_map/ppermute | solution.py:228
  122.1 46.1 %collective-permute-start.8 = (bf16[16,128,256]{2,1,0:T(8,128)(2,1)}, bf16[16,128,256]{2,1,0:T(8,128)(2,1)}, u32[]{:S(2)}, u32[]{:S(2)}) collective-permute-start(bf16[16,128,256]{2,1,0:T(8,128)(2,1)} %copy-done.22), channel_id=1, source_target_pairs={{0,12},{4,8},{8,4},{12,0},{1,13},{5,9},{9,5},{13,1},{2,14},{6,10},... | collective-permute-start | bytes 3145736 | tf_op jit(solution)/shard_map/ppermute | solution.py:228
  122.2 46.9 %collective-permute-start.9 = (bf16[16,128,256]{2,1,0:T(8,128)(2,1)}, bf16[16,128,256]{2,1,0:T(8,128)(2,1)}, u32[]{:S(2)}, u32[]{:S(2)}) collective-permute-start(bf16[16,128,256]{2,1,0:T(8,128)(2,1)} %get-tuple-element.53), channel_id=1, source_target_pairs={{0,4},{4,0},{8,12},{12,8},{1,5},{5,1},{9,13},{13,9},{2,6},{6,2},{1... | collective-permute-start | bytes 3145736 | tf_op jit(solution)/shard_map/ppermute | solution.py:228
  124.3 59.6 %copy-start.3 = (bf16[512,512]{1,0:T(8,128)(2,1)}, bf16[512,512]{1,0:T(8,128)(2,1)S(1)}, u32[]{:S(2)}) copy-start(bf16[512,512]{1,0:T(8,128)(2,1)S(1)} %pad_maximum_fusion.1.k_ref) | copy-start | bytes 1572868
  124.4 70.0 %collective-permute-start.10 = (bf16[16,128,256]{2,1,0:T(8,128)(2,1)S(1)}, bf16[16,128,256]{2,1,0:T(8,128)(2,1)}, u32[]{:S(2)}, u32[]{:S(2)}) collective-permute-start(bf16[16,128,256]{2,1,0:T(8,128)(2,1)S(1)} %get-tuple-element.42.refs_3_), channel_id=1, source_target_pairs={{0,8},{4,12},{8,0},{12,4},{1,9},{5,13},{9,1},{13,5},{2,10},{6,14},... | collective-permute-start | bytes 3145736 | tf_op jit(solution)/shard_map/ppermute | solution.py:228
  125.9 87.3 %collective-permute-start.11 = (bf16[16,128,256]{2,1,0:T(8,128)(2,1)}, bf16[16,128,256]{2,1,0:T(8,128)(2,1)}, u32[]{:S(2)}, u32[]{:S(2)}) collective-permute-start(bf16[16,128,256]{2,1,0:T(8,128)(2,1)} %copy-done.16), channel_id=1, source_target_pairs={{0,12},{4,8},{8,4},{12,0},{1,13},{5,9},{9,5},{13,1},{2,14},{6,10},... | collective-permute-start | bytes 3145736 | tf_op jit(solution)/shard_map/ppermute | solution.py:228
  146.8 89.8 %collective-permute-start.13 = (bf16[16,128,256]{2,1,0:T(8,128)(2,1)}, bf16[16,128,256]{2,1,0:T(8,128)(2,1)S(1)}, u32[]{:S(2)}, u32[]{:S(2)}) collective-permute-start(bf16[16,128,256]{2,1,0:T(8,128)(2,1)} %get-tuple-element.43.refs_9_), channel_id=1, source_target_pairs={{0,8},{4,12},{8,0},{12,4},{1,9},{5,13},{9,1},{13,5},{2,10},{6,14},... | collective-permute-start | bytes 3145736 | tf_op jit(solution)/shard_map/ppermute | solution.py:228
  168.3 54.2 %collective-permute-start.12 = (bf16[16,128,256]{2,1,0:T(8,128)(2,1)}, bf16[16,128,256]{2,1,0:T(8,128)(2,1)S(1)}, u32[]{:S(2)}, u32[]{:S(2)}) collective-permute-start(bf16[16,128,256]{2,1,0:T(8,128)(2,1)} %get-tuple-element.57), channel_id=1, source_target_pairs={{0,4},{4,0},{8,12},{12,8},{1,5},{5,1},{9,13},{13,9},{2,6},{6,2},{1... | collective-permute-start | bytes 3145736 | tf_op jit(solution)/shard_map/ppermute | solution.py:228
  169.1 88.3 %collective-permute-start.14 = (bf16[16,128,256]{2,1,0:T(8,128)(2,1)}, bf16[16,128,256]{2,1,0:T(8,128)(2,1)S(1)}, u32[]{:S(2)}, u32[]{:S(2)}) collective-permute-start(bf16[16,128,256]{2,1,0:T(8,128)(2,1)} %copy-done.13), channel_id=1, source_target_pairs={{0,12},{4,8},{8,4},{12,0},{1,13},{5,9},{9,5},{13,1},{2,14},{6,10},... | collective-permute-start | bytes 3145736 | tf_op jit(solution)/shard_map/ppermute | solution.py:228
  180.9 1.0 copy-start.11
  181.9 1.0 copy-start.12
  182.9 1.1 copy-start.15
  184.0 1.0 copy-start.4
  191.3 1.0 copy-start.7
  192.3 1.0 copy-start.10
  193.3 1.1 copy-start.17
  219.5 1.0 copy-start.5
  220.5 1.0 copy-start.6
  221.5 1.0 copy-start.14
  222.5 35.0 %copy-start.26 = (bf16[16,128,256]{2,1,0:T(8,128)(2,1)}, bf16[16,128,256]{2,1,0:T(8,128)(2,1)S(1)}, u32[]{:S(2)}) copy-start(bf16[16,128,256]{2,1,0:T(8,128)(2,1)S(1)} %collective-permute-done.12.refs_1_) | copy-start | bytes 3145732
  236.6 20.9 %copy-start.25 = (bf16[16,128,256]{2,1,0:T(8,128)(2,1)}, bf16[16,128,256]{2,1,0:T(8,128)(2,1)S(1)}, u32[]{:S(2)}) copy-start(bf16[16,128,256]{2,1,0:T(8,128)(2,1)S(1)} %collective-permute-done.13.refs_2_) | copy-start | bytes 3145732
  257.5 1.0 copy-start.27
  264.9 1.0 copy-start.2
  265.9 1.0 copy-start.8
  266.9 1.0 copy-start.9
  267.9 1.0 copy-start.19
  270.7 1.9 collective-permute-start.16
  273.5 8.8 %collective-permute-start.17 = (f32[256,256]{0,1:T(8,128)S(1)}, f32[256,256]{0,1:T(8,128)}, u32[]{:S(2)}, u32[]{:S(2)}) collective-permute-start(f32[256,256]{0,1:T(8,128)S(1)} %fusion.15), channel_id=1, source_target_pairs={{0,8},{4,12},{8,0},{12,4},{1,9},{5,13},{9,1},{13,5},{2,10},{6,14},... | collective-permute-start | bytes 786440 | tf_op jit(solution)/shard_map/ppermute | solution.py:228
  275.2 35.5 %collective-permute-start.21 = (bf16[16,128,256]{2,1,0:T(8,128)(2,1)}, bf16[16,128,256]{2,1,0:T(8,128)(2,1)}, u32[]{:S(2)}, u32[]{:S(2)}) collective-permute-start(bf16[16,128,256]{2,1,0:T(8,128)(2,1)} %copy-done.15), channel_id=1, source_target_pairs={{0,4},{4,0},{8,12},{12,8},{1,5},{5,1},{9,13},{13,9},{2,6},{6,2},{1... | collective-permute-start | bytes 3145736 | tf_op jit(solution)/shard_map/ppermute | solution.py:228
  275.4 36.7 %collective-permute-start.22 = (bf16[16,128,256]{2,1,0:T(8,128)(2,1)}, bf16[16,128,256]{2,1,0:T(8,128)(2,1)}, u32[]{:S(2)}, u32[]{:S(2)}) collective-permute-start(bf16[16,128,256]{2,1,0:T(8,128)(2,1)} %copy-done.17), channel_id=1, source_target_pairs={{0,4},{4,0},{8,12},{12,8},{1,5},{5,1},{9,13},{13,9},{2,6},{6,2},{1... | collective-permute-start | bytes 3145736 | tf_op jit(solution)/shard_map/ppermute | solution.py:228
  275.8 60.8 %collective-permute-start.23 = (bf16[16,128,256]{2,1,0:T(8,128)(2,1)}, bf16[16,128,256]{2,1,0:T(8,128)(2,1)}, u32[]{:S(2)}, u32[]{:S(2)}) collective-permute-start(bf16[16,128,256]{2,1,0:T(8,128)(2,1)} %copy-done.14), channel_id=1, source_target_pairs={{0,4},{4,0},{8,12},{12,8},{1,5},{5,1},{9,13},{13,9},{2,6},{6,2},{1... | collective-permute-start | bytes 3145736 | tf_op jit(solution)/shard_map/ppermute | solution.py:228
  275.9 62.2 %collective-permute-start.24 = (bf16[16,128,256]{2,1,0:T(8,128)(2,1)}, bf16[16,128,256]{2,1,0:T(8,128)(2,1)}, u32[]{:S(2)}, u32[]{:S(2)}) collective-permute-start(bf16[16,128,256]{2,1,0:T(8,128)(2,1)} %copy-done.19), channel_id=1, source_target_pairs={{0,4},{4,0},{8,12},{12,8},{1,5},{5,1},{9,13},{13,9},{2,6},{6,2},{1... | collective-permute-start | bytes 3145736 | tf_op jit(solution)/shard_map/ppermute | solution.py:228
  282.3 57.4 %collective-permute-start.25 = (bf16[16,128,256]{2,1,0:T(8,128)(2,1)}, bf16[16,128,256]{2,1,0:T(8,128)(2,1)}, u32[]{:S(2)}, u32[]{:S(2)}) collective-permute-start(bf16[16,128,256]{2,1,0:T(8,128)(2,1)} %copy-done.12), channel_id=1, source_target_pairs={{0,8},{4,12},{8,0},{12,4},{1,9},{5,13},{9,1},{13,5},{2,10},{6,14},... | collective-permute-start | bytes 3145736 | tf_op jit(solution)/shard_map/ppermute | solution.py:228
  284.7 0.7 copy-start.23
  310.7 28.9 %collective-permute-start.26 = (bf16[16,128,256]{2,1,0:T(8,128)(2,1)}, bf16[16,128,256]{2,1,0:T(8,128)(2,1)}, u32[]{:S(2)}, u32[]{:S(2)}) collective-permute-start(bf16[16,128,256]{2,1,0:T(8,128)(2,1)} %copy-done.11), channel_id=1, source_target_pairs={{0,12},{4,8},{8,4},{12,0},{1,13},{5,9},{9,5},{13,1},{2,14},{6,10},... | collective-permute-start | bytes 3145736 | tf_op jit(solution)/shard_map/ppermute | solution.py:228
  312.0 45.8 %collective-permute-start.27 = (bf16[16,128,256]{2,1,0:T(8,128)(2,1)}, bf16[16,128,256]{2,1,0:T(8,128)(2,1)}, u32[]{:S(2)}, u32[]{:S(2)}) collective-permute-start(bf16[16,128,256]{2,1,0:T(8,128)(2,1)} %copy-done.10), channel_id=1, source_target_pairs={{0,8},{4,12},{8,0},{12,4},{1,9},{5,13},{9,1},{13,5},{2,10},{6,14},... | collective-permute-start | bytes 3145736 | tf_op jit(solution)/shard_map/ppermute | solution.py:228
  336.6 44.9 %collective-permute-start.28 = (bf16[16,128,256]{2,1,0:T(8,128)(2,1)}, bf16[16,128,256]{2,1,0:T(8,128)(2,1)}, u32[]{:S(2)}, u32[]{:S(2)}) collective-permute-start(bf16[16,128,256]{2,1,0:T(8,128)(2,1)} %copy-done.7), channel_id=1, source_target_pairs={{0,12},{4,8},{8,4},{12,0},{1,13},{5,9},{9,5},{13,1},{2,14},{6,10},... | collective-permute-start | bytes 3145736 | tf_op jit(solution)/shard_map/ppermute | solution.py:228
  338.1 115.9 %collective-permute-start.18 = (bf16[16,128,256]{2,1,0:T(8,128)(2,1)}, bf16[16,128,256]{2,1,0:T(8,128)(2,1)}, u32[]{:S(2)}, u32[]{:S(2)}) collective-permute-start(bf16[16,128,256]{2,1,0:T(8,128)(2,1)} %copy-done.9), channel_id=1, source_target_pairs={{0,8},{4,12},{8,0},{12,4},{1,9},{5,13},{9,1},{13,5},{2,10},{6,14},... | collective-permute-start | bytes 3145736 | tf_op jit(solution)/shard_map/ppermute | solution.py:228
  339.6 111.2 %collective-permute-start.19 = (bf16[16,128,256]{2,1,0:T(8,128)(2,1)}, bf16[16,128,256]{2,1,0:T(8,128)(2,1)}, u32[]{:S(2)}, u32[]{:S(2)}) collective-permute-start(bf16[16,128,256]{2,1,0:T(8,128)(2,1)} %copy-done.5), channel_id=1, source_target_pairs={{0,12},{4,8},{8,4},{12,0},{1,13},{5,9},{9,5},{13,1},{2,14},{6,10},... | collective-permute-start | bytes 3145736 | tf_op jit(solution)/shard_map/ppermute | solution.py:228
  339.7 108.1 %collective-permute-start.20 = (bf16[16,128,256]{2,1,0:T(8,128)(2,1)}, bf16[16,128,256]{2,1,0:T(8,128)(2,1)}, u32[]{:S(2)}, u32[]{:S(2)}) collective-permute-start(bf16[16,128,256]{2,1,0:T(8,128)(2,1)} %copy-done.6), channel_id=1, source_target_pairs={{0,8},{4,12},{8,0},{12,4},{1,9},{5,13},{9,1},{13,5},{2,10},{6,14},... | collective-permute-start | bytes 3145736 | tf_op jit(solution)/shard_map/ppermute | solution.py:228
  357.9 112.8 %collective-permute-start.15 = (bf16[16,128,256]{2,1,0:T(8,128)(2,1)}, bf16[16,128,256]{2,1,0:T(8,128)(2,1)S(1)}, u32[]{:S(2)}, u32[]{:S(2)}) collective-permute-start(bf16[16,128,256]{2,1,0:T(8,128)(2,1)} %copy-done.8), channel_id=1, source_target_pairs={{0,12},{4,8},{8,4},{12,0},{1,13},{5,9},{9,5},{13,1},{2,14},{6,10},... | collective-permute-start | bytes 3145736 | tf_op jit(solution)/shard_map/ppermute | solution.py:228

commit v2 on v1

--- a/solution.py
+++ b/solution.py
@@ -42,12 +42,12 @@
             outs[part][first : first + TILE] = done.reshape(group.shape)
 
 
-def apply_y(walker, kinetic, bases, rows, after):
-    own, depth, orbitals = walker.shape
+def apply_y(walker, kinetic, bases, rows, start, own, after):
+    _, depth, orbitals = walker.shape
     parts = len(bases)
     every = rows * parts
     specs = [pl.BlockSpec((rows, depth), lambda i, b, p=p: (b[p], 0)) for p in range(parts)]
-    specs.append(pl.BlockSpec((TILE, depth, orbitals), lambda i, b: (i, 0, 0)))
+    specs.append(pl.BlockSpec((TILE, depth, orbitals), lambda i, b: (i + start // TILE, 0, 0)))
     operands = [kinetic] * parts + [walker]
     if after is not None:
         specs.append(pl.BlockSpec(memory_space=pl.ANY))
@@ -76,7 +76,7 @@
 
 
 def x_body(count, lines, own, k_ref, f_ref, g_ref, *refs):
-    ins, outs, gram = refs[:count], refs[count : 2 * count], refs[2 * count]
+    ins, outs, gram = refs[: -count - 1], refs[-count - 1 : -1], refs[-1]
 
     @pl.when(pl.program_id(0) == 0)
     def _():
@@ -97,9 +97,14 @@
 
 def apply_x(columns, kinetic, factor, gram, lines):
     count = len(columns)
-    rows, own, orbitals = columns[0].shape
-    every = count * own
-    block = pl.BlockSpec((lines, own, orbitals), lambda i: (i, 0, 0))
+    columns = [piece for pieces in columns for piece in pieces]
+    rows, _, orbitals = columns[0].shape
+    every = kinetic.shape[0]
+    own = every // count
+
+    def block(sites):
+        return pl.BlockSpec((lines, sites, orbitals), lambda i: (i, 0, 0))
+
     outs = pl.pallas_call(
         functools.partial(x_body, count, lines, own),
         grid=(rows // lines,),
@@ -108,8 +113,8 @@
             pl.BlockSpec((1, every, lines), lambda i: (i, 0, 0)),
             pl.BlockSpec((orbitals, orbitals), lambda i: (0, 0)),
         ]
-        + [block] * count,
-        out_specs=[block] * count + [pl.BlockSpec((orbitals, orbitals), lambda i: (0, 0))],
+        + [block(column.shape[1]) for column in columns],
+        out_specs=[block(own)] * count + [pl.BlockSpec((orbitals, orbitals), lambda i: (0, 0))],
         out_shape=[jax.ShapeDtypeStruct((rows, own, orbitals), jnp.bfloat16)] * count
         + [jax.ShapeDtypeStruct((orbitals, orbitals), jnp.float32)],
         compiler_params=pltpu.CompilerParams(vmem_limit_bytes=VMEM),
@@ -199,12 +204,13 @@
 
 
 def factorize(gram):
-    half = gram.shape[-1] // 2
+    half = gram.shape[-1]
+    top, side, bottom = gram[:half], gram[half : 2 * half], gram[2 * half :]
     upper = jnp.zeros((half, half), jnp.float32)
-    first = jnp.linalg.cholesky(gram[:half, :half])
+    first = jnp.linalg.cholesky(top)
     first_inverse = small_inverse(first)
-    below = times(gram[half:, :half], first_inverse.T)
-    second = jnp.linalg.cholesky(gram[half:, half:] - times(below, below.T))
+    below = times(side, first_inverse.T)
+    second = jnp.linalg.cholesky(bottom - times(below, below.T))
     second_inverse = small_inverse(second)
     corner = -times(second_inverse, times(below, first_inverse))
     lower = jnp.block([[first, upper], [below, second]])
@@ -230,16 +236,16 @@
     def base(d, c):
         return (me ^ d) * share + c * rows
 
-    blocks = [[None] * count for _ in range(chunks)]
+    blocks = [[[] for _ in range(count)] for _ in range(chunks)]
     sent = [None]
-    for c in range(chunks):
-        sent = apply_y(walker, kinetic_y, [base(d, c) for d in far], rows, sent[0])
+    for c, start, sites in early_pieces(own, chunks):
+        sent = apply_y(walker, kinetic_y, [base(d, c) for d in far], rows, start, sites, sent[0])
         for d, value in zip(far, sent):
-            blocks[c][d] = swap(value, d)
+            blocks[c][d].append(swap(value, d))
     pairs = [(d, c) for c in range(chunks) for d in near]
-    sent = apply_y(walker, kinetic_y, [base(d, c) for d, c in pairs], rows, sent[0])
+    sent = apply_y(walker, kinetic_y, [base(d, c) for d, c in pairs], rows, 0, own, sent[0])
     for (d, c), value in zip(pairs, sent):
-        blocks[c][d] = swap(value, d)
+        blocks[c][d].append(swap(value, d))
 
     fields = [
         swap(lax.dynamic_slice_in_dim(field, (me ^ d) * share, share, 1), d)
@@ -261,10 +267,23 @@
         outs, gram = apply_x(blocks[c], order, factor[c * per : (c + 1) * per], gram, lines)
         scaled.append(outs)
     gram = gram * (1.0 / (count * own * depth))
-    step = 1
+    half = orbitals // 2
+    gram = jnp.concatenate([gram[:half, :half], gram[half:, :half], gram[half:, half:]], axis=0)
+    gram = gram + swap(gram, 1)
+    core = me % CORES
+    size = gram.shape[0] // CORES
+    mine = lax.dynamic_slice_in_dim(gram, core * size, size, 0)
+    step = CORES
     while step < count:
-        gram = gram + swap(gram, step)
+        arrived = swap(mine, step)
+        mine = mine + arrived
         step *= 2
+    other = swap(mine, 1)
+    gram = jnp.where(
+        core == 0,
+        jnp.concatenate([mine, other], axis=0),
+        jnp.concatenate([other, mine], axis=0),
+    )
 
     home = [[swap(scaled[c][e], e) for e in range(count)] for c in range(chunks)]
     lower, inverse = factorize(gram)
@@ -288,6 +307,12 @@
     return jnp.concatenate(results, axis=0), jnp.concatenate(lowers, axis=0)
 
 
+def early_pieces(own, chunks):
+    cut = own // 4
+    whole = [(c, 0, own) for c in range(chunks)]
+    return ([(0, 0, cut), (0, cut, own - cut)] + whole[1:]) if cut % TILE == 0 else whole
+
+
 def solution(mesh):
     count = mesh.shape["site"]
     placed = (

time: 474 us -> 433 us (0.914)
  waiting for transfers between devices: 233 us -> 186 us
  local copies, waits for them, and re-layouts: 33.4 us -> 38.4 us
    ppermute x29 -> x32, waiting for transfers between devices: 233 us -> 186 us  [swap(): return lax.ppermute(value, 'site', [(s, s ^ d) for s in range(count)])]
    pallas_call x5 -> x6, Pallas kernels: 58.3 us -> 60.2 us  [apply_y(): pl.pallas_call(functools.partial(y_body, parts, rows, TILE), grid_spec=pl...]
    unnamed x57 -> x59, local copies, waits for them, and re-layouts: 22.8 us -> 21.7 us
    ppermute x29 -> x32, starting transfers between devices: 24.3 us -> 24.3 us  [swap(): return lax.ppermute(value, 'site', [(s, s ^ d) for s in range(count)])]
  transfers between devices with their start and end apart: 29 -> 32, of which waited for: 14 -> 12; matrix products, arithmetic and copies ran while one was open for 14% -> 15% of each run, Pallas kernels for 12% -> 27%
where the time goes in v2:
time: 433 us; the launch traced here: 432 us
  waiting for transfers between devices  186 us (43%)
  Pallas kernels  127 us (29%)
  other arithmetic  53.2 us (12%)
  local copies, waits for them, and re-layouts  38.4 us (9%)
  starting transfers between devices  24.3 us (6%)
    ppermute x32, waiting for transfers between devices, swap(): return lax.ppermute(value, 'site', [(s, s ^ d) for s in range(count)])  186 us
    pallas_call x6, Pallas kernels, apply_y(): pl.pallas_call(functools.partial(y_body, parts, rows, TILE), grid_spec=pl...  60.2 us
    pallas_call x5, Pallas kernels, orthonormal_rows(): pl.pallas_call(functools.partial(out_body, parts, steps, sites), grid_spe...  40.9 us
    pallas_call x4, Pallas kernels, apply_x(): pl.pallas_call(functools.partial(x_body, count, lines, own), grid=(rows /...  26.1 us
    ppermute x32, starting transfers between devices, swap(): return lax.ppermute(value, 'site', [(s, s ^ d) for s in range(count)])  24.3 us
    another operation x4, other arithmetic, small_inverse(): return jax.scipy.linalg.solve_triangular(lower, identity, lower=True)  21.7 us
    unnamed x59, local copies, waits for them, and re-layouts  21.7 us
    another operation x3, other arithmetic, factorize(): second = jnp.linalg.cholesky(bottom - times(below, below.T))  12.4 us
  transfers between devices with their start and end apart: 32, of which 12 were waited for; matrix products, arithmetic and copies ran while one was open for 15% of the time, Pallas kernels for 27%

profile of v2, /device:TPU:0, one launch (start us, length us, event | category | flops | bytes accessed | tf_op | source)
XLA Modules:
  0.0 431.7 jit_solution(16078894015260605058)
XLA Ops:
  0.7 1.6 constant_dynamic-slice_fusion.3
  2.9 2.4 collective-permute-start.2
  7.6 3.6 apply_y.6
  11.9 1.5 collective-permute-start.4
  13.3 9.2 %apply_y.7 = (bf16[16,96,256]{2,1,0:T(8,128)(2,1)S(1)}, bf16[16,96,256]{2,1,0:T(8,128)(2,1)}) custom-call(s32[2]{0:T(128)S(1)} %get-tuple-element.100.base_ref, bf16[256,256]{1,0:T(8,128)(2,1)S(1)} %copy-done, bf16[256,256]{1,0:T(8,128)(2,1)S(1)} %copy-done, bf16[128,256,256]{2,1,0:T(8,128)(2,1)} %bitcast.59, bf16[16,32,256]{2,1,0:T(8,128)(2,1)S(1)} %get-tuple-element.42.refs_3_), custom_call_target="tpu_custom_call" | custom-call | flops 402653184 | bytes 14155776 | tf_op jit(solution)/shard_map/apply_y/pallas_call | solution.py:55
  24.1 11.6 %apply_y.8 = (bf16[16,128,256]{2,1,0:T(8,128)(2,1)S(1)}, bf16[16,128,256]{2,1,0:T(8,128)(2,1)}) custom-call(s32[2]{0:T(128)S(1)} %get-tuple-element.101.base_ref, bf16[256,256]{1,0:T(8,128)(2,1)S(1)} %copy-done.1, bf16[256,256]{1,0:T(8,128)(2,1)S(1)} %copy-done.1, bf16[128,256,256]{2,1,0:T(8,128)(2,1)} %bitcast.60, ...), custom_call_target="tpu_custom_call" | custom-call | flops 536870912 | bytes 18874368 | tf_op jit(solution)/shard_map/apply_y/pallas_call | solution.py:55
  35.8 10.9 %apply_y.9 = (bf16[16,128,256]{2,1,0:T(8,128)(2,1)S(1)}, bf16[16,128,256]{2,1,0:T(8,128)(2,1)S(1)}) custom-call(s32[2]{0:T(128)S(1)} %get-tuple-element.102.base_ref, bf16[256,256]{1,0:T(8,128)(2,1)S(1)} %copy-done.1, bf16[256,256]{1,0:T(8,128)(2,1)S(1)} %copy-done.1, bf16[128,256,256]{2,1,0:T(8,128)(2,1)} %bitcast.61, ...), custom_call_target="tpu_custom_call" | custom-call | flops 536870912 | bytes 18874368 | tf_op jit(solution)/shard_map/apply_y/pallas_call | solution.py:55
  46.7 1.0 copy-done.16
  47.7 11.7 %apply_y.10 = (bf16[16,128,256]{2,1,0:T(8,128)(2,1)}, bf16[16,128,256]{2,1,0:T(8,128)(2,1)S(1)}) custom-call(s32[2]{0:T(128)S(1)} %get-tuple-element.103.base_ref, bf16[256,256]{1,0:T(8,128)(2,1)S(1)} %copy-done.1, bf16[256,256]{1,0:T(8,128)(2,1)S(1)} %copy-done.1, bf16[128,256,256]{2,1,0:T(8,128)(2,1)} %bitcast.62, ...), custom_call_target="tpu_custom_call" | custom-call | flops 536870912 | bytes 18874368 | tf_op jit(solution)/shard_map/apply_y/pallas_call | solution.py:55
  59.4 1.0 copy-done.15
  60.3 1.4 copy.33
  62.7 13.3 %apply_y.11 = (bf16[16,128,256]{2,1,0:T(8,128)(2,1)S(1)}, bf16[16,128,256]{2,1,0:T(8,128)(2,1)}, bf16[16,128,256]{2,1,0:T(8,128)(2,1)S(1)}, bf16[16,128,256]{2,1...) custom-call(s32[8]{0:T(128)S(1)} %and_select_fusion.5.base_ref, ...), custom_call_target="tpu_custom_call" | custom-call | flops 2147483648 | bytes 25165824 | tf_op jit(solution)/shard_map/apply_y/pallas_call | solution.py:55
  77.0 1.0 copy-done.18
  80.2 1.5 collective-permute-start.9
  83.8 1.1 constant_dynamic-slice_fusion.11
  87.4 1.5 collective-permute-start.12
  89.6 2.7 copy.40
  92.3 14.0 %collective-permute-done.9.refs_2_ = bf16[16,128,256]{2,1,0:T(8,128)(2,1)} collective-permute-done((bf16[16,128,256]{2,1,0:T(8,128)(2,1)S(1)}, bf16[16,128,256]{2,1,0:T(8,128)(2,1)}, u32[]{:S(2)}, u32[]{:S(2)}) %collective-permute-start.9) | collective-permute-done | bytes 1048608 | tf_op jit(solution)/shard_map/ppermute | solution.py:234
  106.3 1.5 collective-permute-start.15
  107.8 20.0 %collective-permute-done.10.refs_3_ = bf16[16,128,256]{2,1,0:T(8,128)(2,1)} collective-permute-done((bf16[16,128,256]{2,1,0:T(8,128)(2,1)}, bf16[16,128,256]{2,1,0:T(8,128)(2,1)}, u32[]{:S(2)}, u32[]{:S(2)}) %collective-permute-start.10) | collective-permute-done | bytes 1048608 | tf_op jit(solution)/shard_map/ppermute | solution.py:234
  128.6 1.1 collective-permute-start.16
  129.7 4.2 fusion.18
  133.9 6.9 %apply_x.4 = (bf16[16,128,256]{2,1,0:T(8,128)(2,1)S(1)}, bf16[16,128,256]{2,1,0:T(8,128)(2,1)S(1)}, bf16[16,128,256]{2,1,0:T(8,128)(2,1)}, bf16[16,128,256]{2,1,0:T(8,128)(2,1)}, f32[256,256]{1,0:T(8,128)S(1)}) custom-call(bf16[512,512]{1,0:T(8,128)(2,1)S(1)} %pad_maximum_fusion.1.k_ref, f32[4,512,4]{2,1,0:T(8,128)} %get-tuple-element.84.f_ref, ...), custom_call_target="tpu_custom_call" | custom-call | flops 3221225472 | bytes 8388608 | tf_op jit(solution)/shard_map/apply_x/pallas_call | solution.py:108
  141.8 1.0 copy-done.4
  142.8 6.3 %apply_x.5 = (bf16[16,128,256]{2,1,0:T(8,128)(2,1)S(1)}, bf16[16,128,256]{2,1,0:T(8,128)(2,1)S(1)}, bf16[16,128,256]{2,1,0:T(8,128)(2,1)S(1)}, bf16[16,128,256]{2,1,0:T(8,128)(2,1)S(1)}, f32[256,256]{1,0:T(8,128)S(1)}) custom-call(bf16[512,512]{1,0:T(8,128)(2,1)S(1)} %copy-done.4, f32[4,512,4]{2,1,0:T(8,128)} %get-tuple-element.85.f_ref, ...), custom_call_target="tpu_custom_call" | custom-call | flops 3221225472 | bytes 8388608 | tf_op jit(solution)/shard_map/apply_x/pallas_call | solution.py:108
  149.2 1.0 copy-done.7
  150.2 1.0 copy-done.10
  151.2 1.0 copy-done.13
  152.2 20.5 %collective-permute-done.13.refs_3_ = bf16[16,128,256]{2,1,0:T(8,128)(2,1)} collective-permute-done((bf16[16,128,256]{2,1,0:T(8,128)(2,1)}, bf16[16,128,256]{2,1,0:T(8,128)(2,1)}, u32[]{:S(2)}, u32[]{:S(2)}) %collective-permute-start.13) | collective-permute-done | bytes 1048608 | tf_op jit(solution)/shard_map/ppermute | solution.py:234
  172.7 6.3 %apply_x.6 = (bf16[16,128,256]{2,1,0:T(8,128)(2,1)S(1)}, bf16[16,128,256]{2,1,0:T(8,128)(2,1)S(1)}, bf16[16,128,256]{2,1,0:T(8,128)(2,1)S(1)}, bf16[16,128,256]{2,1,0:T(8,128)(2,1)S(1)}, f32[256,256]{1,0:T(8,128)S(1)}) custom-call(bf16[512,512]{1,0:T(8,128)(2,1)S(1)} %copy-done.4, f32[4,512,4]{2,1,0:T(8,128)} %get-tuple-element.86.f_ref, ...), custom_call_target="tpu_custom_call" | custom-call | flops 3221225472 | bytes 8388608 | tf_op jit(solution)/shard_map/apply_x/pallas_call | solution.py:108
  179.0 1.0 copy-done.5
  181.0 1.0 copy-done.12
  182.0 14.0 %collective-permute-done.15.refs_2_ = bf16[16,128,256]{2,1,0:T(8,128)(2,1)S(1)} collective-permute-done((bf16[16,128,256]{2,1,0:T(8,128)(2,1)}, bf16[16,128,256]{2,1,0:T(8,128)(2,1)S(1)}, u32[]{:S(2)}, u32[]{:S(2)}) %collective-permute-start.15) | collective-permute-done | bytes 1048608 | tf_op jit(solution)/shard_map/ppermute | solution.py:234
  196.1 21.4 %collective-permute-done.16.refs_3_ = bf16[16,128,256]{2,1,0:T(8,128)(2,1)S(1)} collective-permute-done((bf16[16,128,256]{2,1,0:T(8,128)(2,1)}, bf16[16,128,256]{2,1,0:T(8,128)(2,1)S(1)}, u32[]{:S(2)}, u32[]{:S(2)}) %collective-permute-start.16) | collective-permute-done | bytes 1048608 | tf_op jit(solution)/shard_map/ppermute | solution.py:234
  217.5 1.0 copy-done.28
  218.5 6.5 %apply_x.7 = (bf16[16,128,256]{2,1,0:T(8,128)(2,1)S(1)}, bf16[16,128,256]{2,1,0:T(8,128)(2,1)S(1)}, bf16[16,128,256]{2,1,0:T(8,128)(2,1)S(1)}, bf16[16,128,256]{2,1,0:T(8,128)(2,1)S(1)}, f32[256,256]{1,0:T(8,128)S(1)}) custom-call(bf16[512,512]{1,0:T(8,128)(2,1)S(1)} %copy-done.4, f32[4,512,4]{2,1,0:T(8,128)} %get-tuple-element.87.f_ref, ...), custom_call_target="tpu_custom_call" | custom-call | flops 3221225472 | bytes 8388608 | tf_op jit(solution)/shard_map/apply_x/pallas_call | solution.py:108
  225.0 1.0 copy-done.2
  226.0 1.0 copy-done.8
  227.0 1.0 copy-done.9
  228.0 1.0 copy-done.14
  231.3 1.2 collective-permute-done.18
  232.5 1.1 fusion.4
  233.6 1.5 collective-permute-start.19
  235.2 4.2 collective-permute-done.19
  242.4 1.5 collective-permute-start.28
  243.9 1.1 maximum_select_fusion
  245.1 11.7 %cholesky.44 = f32[128,128]{1,0:T(8,128)S(1)} custom-call(f32[128,128]{1,0:T(8,128)S(1)} %fusion.15), custom_call_target="Cholesky" | custom-call | tf_op jit(solution)/shard_map/jit(cholesky)/cholesky | solution.py:210
  257.5 1.3 select_bitcast_fusion.1
  258.8 9.8 %custom-call.6 = f32[1,128,128]{1,2,0:T(8,128)S(1)} custom-call(f32[1,128,128]{2,1,0:T(8,128)S(1)} %get-tuple-element.82), custom_call_target="InvertDiagBlocksLowerTriangular" | custom-call | tf_op jit(solution)/shard_map/jit(_solve_triangular)/triangular_solve | solution.py:203
  269.7 1.5 collective-permute-start.30
  271.3 11.7 %cholesky.55 = f32[128,128]{1,0:T(8,128)S(1)} custom-call(f32[128,128]{1,0:T(8,128)S(1)} %fusion.13), custom_call_target="Cholesky" | custom-call | tf_op jit(solution)/shard_map/jit(cholesky)/cholesky | solution.py:213
  284.3 10.0 %custom-call.7 = f32[1,128,128]{1,2,0:T(8,128)S(1)} custom-call(f32[1,128,128]{2,1,0:T(8,128)S(1)} %get-tuple-element.80), custom_call_target="InvertDiagBlocksLowerTriangular" | custom-call | tf_op jit(solution)/shard_map/jit(_solve_triangular)/triangular_solve | solution.py:203
  295.1 1.5 collective-permute-start.21
  296.8 1.5 collective-permute-start.23
  298.7 18.9 %collective-permute-done.30.refs_10_ = bf16[16,128,256]{2,1,0:T(8,128)(2,1)} collective-permute-done((bf16[16,128,256]{2,1,0:T(8,128)(2,1)}, bf16[16,128,256]{2,1,0:T(8,128)(2,1)}, u32[]{:S(2)}, u32[]{:S(2)}) %collective-permute-start.30) | collective-permute-done | bytes 1048608 | tf_op jit(solution)/shard_map/ppermute | solution.py:234
  317.9 1.6 fusion.1
  319.5 20.3 %collective-permute-done.31.refs_11_ = bf16[16,128,256]{2,1,0:T(8,128)(2,1)} collective-permute-done((bf16[16,128,256]{2,1,0:T(8,128)(2,1)}, bf16[16,128,256]{2,1,0:T(8,128)(2,1)}, u32[]{:S(2)}, u32[]{:S(2)}) %collective-permute-start.31) | collective-permute-done | bytes 1048608 | tf_op jit(solution)/shard_map/ppermute | solution.py:234
  339.7 29.4 %orthonormal_rows.5.refs_2_ = bf16[128,256,256]{2,1,0:T(8,128)(2,1)} custom-call(s32[12]{0:T(128)S(1)} %and_select_fusion.base_ref, bf16[16,128,256]{2,1,0:T(8,128)(2,1)S(1)} %get-tuple-element.68.refs_0_, bf16[16,128,256]{2,1,0:T(8,128)(2,1)} %collective-permute-done.24.refs_1_, bf16[16,128,256]{2,1,0:T(8,128)(2,1)S(1)} %get-tuple-element.70.refs_2_, ...), custom_call_target="tpu_custom_call" | custom-call | flops 3221225472 | bytes 25165824 | tf_op jit(solution)/shard_map/orthonormal_rows/pallas_call | solution.py:173
  369.1 38.4 %collective-permute-done.23.refs_0_ = bf16[16,128,256]{2,1,0:T(8,128)(2,1)} collective-permute-done((bf16[16,128,256]{2,1,0:T(8,128)(2,1)}, bf16[16,128,256]{2,1,0:T(8,128)(2,1)}, u32[]{:S(2)}, u32[]{:S(2)}) %collective-permute-start.23) | collective-permute-done | bytes 1048608 | tf_op jit(solution)/shard_map/ppermute | solution.py:234
  407.5 3.1 orthonormal_rows.6.refs_2_
  410.6 3.1 orthonormal_rows.7.refs_2_
  413.7 3.1 orthonormal_rows.8.refs_2_
  416.8 12.7 %collective-permute-done.17.refs_0_ = bf16[16,128,256]{2,1,0:T(8,128)(2,1)S(1)} collective-permute-done((bf16[16,128,256]{2,1,0:T(8,128)(2,1)}, bf16[16,128,256]{2,1,0:T(8,128)(2,1)S(1)}, u32[]{:S(2)}, u32[]{:S(2)}) %collective-permute-start.17) | collective-permute-done | bytes 1048608 | tf_op jit(solution)/shard_map/ppermute | solution.py:234
  429.5 2.2 orthonormal_rows.9
  (130 shorter events, 27.7 us)
Async XLA Ops:
  2.9 58.9 %collective-permute-start.2 = (bf16[128,64]{0,1:T(8,128)(2,1)}, bf16[128,64]{0,1:T(8,128)(2,1)}, u32[]{:S(2)}, u32[]{:S(2)}) collective-permute-start(bf16[128,64]{0,1:T(8,128)(2,1)} %bitcast.6), channel_id=1, source_target_pairs={{0,12},{4,8},{8,4},{12,0},{1,13},{5,9},{9,5},{13,1},{2,14},{6,10},... | collective-permute-start | bytes 49160 | tf_op jit(solution)/shard_map/ppermute | solution.py:234
  6.0 56.5 %collective-permute-start.1 = (bf16[128,64]{0,1:T(8,128)(2,1)}, bf16[128,64]{0,1:T(8,128)(2,1)}, u32[]{:S(2)}, u32[]{:S(2)}) collective-permute-start(bf16[128,64]{0,1:T(8,128)(2,1)} %bitcast.4), channel_id=1, source_target_pairs={{0,8},{4,12},{8,0},{12,4},{1,9},{5,13},{9,1},{13,5},{2,10},{6,14},... | collective-permute-start | bytes 49160 | tf_op jit(solution)/shard_map/ppermute | solution.py:234
  6.7 0.9 copy-start
  7.6 16.5 %copy-start.1 = (bf16[256,256]{1,0:T(8,128)(2,1)S(1)}, bf16[256,256]{1,0:T(8,128)(2,1)}, u32[]{:S(2)}) copy-start(bf16[256,256]{1,0:T(8,128)(2,1)} %refs_7_.1) | copy-start | bytes 393220
  11.2 0.7 copy-start.22
  11.9 67.5 %collective-permute-start.4 = (bf16[16,32,256]{2,1,0:T(8,128)(2,1)S(1)}, bf16[16,32,256]{2,1,0:T(8,128)(2,1)S(1)}, u32[]{:S(2)}, u32[]{:S(2)}) collective-permute-start(bf16[16,32,256]{2,1,0:T(8,128)(2,1)S(1)} %get-tuple-element.42.refs_3_), channel_id=1, source_target_pairs={{0,8},{4,12},{8,0},{12,4},{1,9},{5,13},{9,1},{13,5},{2,10},{6,14},... | collective-permute-start | bytes 786440 | tf_op jit(solution)/shard_map/ppermute | solution.py:234
  22.5 59.1 %collective-permute-start.5 = (bf16[16,96,256]{2,1,0:T(8,128)(2,1)S(1)}, bf16[16,96,256]{2,1,0:T(8,128)(2,1)}, u32[]{:S(2)}, u32[]{:S(2)}) collective-permute-start(bf16[16,96,256]{2,1,0:T(8,128)(2,1)S(1)} %get-tuple-element.43.refs_3_), channel_id=1, source_target_pairs={{0,8},{4,12},{8,0},{12,4},{1,9},{5,13},{9,1},{13,5},{2,10},{6,14},... | collective-permute-start | bytes 2359304 | tf_op jit(solution)/shard_map/ppermute | solution.py:234
  23.1 58.9 %collective-permute-start.7 = (bf16[16,96,256]{2,1,0:T(8,128)(2,1)}, bf16[16,96,256]{2,1,0:T(8,128)(2,1)}, u32[]{:S(2)}, u32[]{:S(2)}) collective-permute-start(bf16[16,96,256]{2,1,0:T(8,128)(2,1)} %get-tuple-element.50), channel_id=1, source_target_pairs={{0,12},{4,8},{8,4},{12,0},{1,13},{5,9},{9,5},{13,1},{2,14},{6,10},... | collective-permute-start | bytes 2359304 | tf_op jit(solution)/shard_map/ppermute | solution.py:234
  46.7 1.0 copy-start.16
  59.4 1.0 copy-start.15
  61.8 17.1 %collective-permute-start = (bf16[128,64]{0,1:T(8,128)(2,1)}, bf16[128,64]{0,1:T(8,128)(2,1)S(1)}, u32[]{:S(2)}, u32[]{:S(2)}) collective-permute-start(bf16[128,64]{0,1:T(8,128)(2,1)} %bitcast.68), channel_id=1, source_target_pairs={{0,4},{4,0},{8,12},{12,8},{1,5},{5,1},{9,13},{13,9},{2,6},{6,2},{1... | collective-permute-start | bytes 49160 | tf_op jit(solution)/shard_map/ppermute | solution.py:234
  62.5 17.0 %collective-permute-start.6 = (bf16[16,32,256]{2,1,0:T(8,128)(2,1)}, bf16[16,32,256]{2,1,0:T(8,128)(2,1)S(1)}, u32[]{:S(2)}, u32[]{:S(2)}) collective-permute-start(bf16[16,32,256]{2,1,0:T(8,128)(2,1)} %copy-done.22), channel_id=1, source_target_pairs={{0,12},{4,8},{8,4},{12,0},{1,13},{5,9},{9,5},{13,1},{2,14},{6,10},... | collective-permute-start | bytes 786440 | tf_op jit(solution)/shard_map/ppermute | solution.py:234
  76.0 1.0 copy-start.17
  77.0 1.0 copy-start.18
  78.0 1.0 copy-start.19
  78.9 2.7 copy-start.25
  78.9 8.5 %collective-permute-start.3 = (bf16[16,128,256]{2,1,0:T(8,128)(2,1)}, bf16[16,128,256]{2,1,0:T(8,128)(2,1)}, u32[]{:S(2)}, u32[]{:S(2)}) collective-permute-start(bf16[16,128,256]{2,1,0:T(8,128)(2,1)} %get-tuple-element.48), channel_id=1, source_target_pairs={{0,4},{4,0},{8,12},{12,8},{1,5},{5,1},{9,13},{13,9},{2,6},{6,2},{1... | collective-permute-start | bytes 3145736 | tf_op jit(solution)/shard_map/ppermute | solution.py:234
  79.4 9.5 %collective-permute-start.8 = (bf16[16,128,256]{2,1,0:T(8,128)(2,1)}, bf16[16,128,256]{2,1,0:T(8,128)(2,1)}, u32[]{:S(2)}, u32[]{:S(2)}) collective-permute-start(bf16[16,128,256]{2,1,0:T(8,128)(2,1)} %get-tuple-element.53), channel_id=1, source_target_pairs={{0,4},{4,0},{8,12},{12,8},{1,5},{5,1},{9,13},{13,9},{2,6},{6,2},{1... | collective-permute-start | bytes 3145736 | tf_op jit(solution)/shard_map/ppermute | solution.py:234
  79.5 0.7 copy-start.20
  80.2 26.1 %collective-permute-start.9 = (bf16[16,128,256]{2,1,0:T(8,128)(2,1)S(1)}, bf16[16,128,256]{2,1,0:T(8,128)(2,1)}, u32[]{:S(2)}, u32[]{:S(2)}) collective-permute-start(bf16[16,128,256]{2,1,0:T(8,128)(2,1)S(1)} %get-tuple-element.44.refs_3_), channel_id=1, source_target_pairs={{0,8},{4,12},{8,0},{12,4},{1,9},{5,13},{9,1},{13,5},{2,10},{6,14},... | collective-permute-start | bytes 3145736 | tf_op jit(solution)/shard_map/ppermute | solution.py:234
  81.6 52.3 %copy-start.21 = (bf16[16,32,256]{2,1,0:T(8,128)(2,1)S(1)}, bf16[16,32,256]{2,1,0:T(8,128)(2,1)}, u32[]{:S(2)}) copy-start(bf16[16,32,256]{2,1,0:T(8,128)(2,1)} %copy-done.20) | copy-start | bytes 786436
  81.6 46.1 %collective-permute-start.10 = (bf16[16,128,256]{2,1,0:T(8,128)(2,1)}, bf16[16,128,256]{2,1,0:T(8,128)(2,1)}, u32[]{:S(2)}, u32[]{:S(2)}) collective-permute-start(bf16[16,128,256]{2,1,0:T(8,128)(2,1)} %get-tuple-element.54), channel_id=1, source_target_pairs={{0,12},{4,8},{8,4},{12,0},{1,13},{5,9},{9,5},{13,1},{2,14},{6,10},... | collective-permute-start | bytes 3145736 | tf_op jit(solution)/shard_map/ppermute | solution.py:234
  82.0 46.6 %collective-permute-start.11 = (bf16[16,128,256]{2,1,0:T(8,128)(2,1)}, bf16[16,128,256]{2,1,0:T(8,128)(2,1)}, u32[]{:S(2)}, u32[]{:S(2)}) collective-permute-start(bf16[16,128,256]{2,1,0:T(8,128)(2,1)} %get-tuple-element.57), channel_id=1, source_target_pairs={{0,4},{4,0},{8,12},{12,8},{1,5},{5,1},{9,13},{13,9},{2,6},{6,2},{1... | collective-permute-start | bytes 3145736 | tf_op jit(solution)/shard_map/ppermute | solution.py:234
  85.2 56.6 %copy-start.3 = (bf16[512,512]{1,0:T(8,128)(2,1)}, bf16[512,512]{1,0:T(8,128)(2,1)S(1)}, u32[]{:S(2)}) copy-start(bf16[512,512]{1,0:T(8,128)(2,1)S(1)} %pad_maximum_fusion.1.k_ref) | copy-start | bytes 1572868
  87.4 64.8 %collective-permute-start.12 = (bf16[16,128,256]{2,1,0:T(8,128)(2,1)S(1)}, bf16[16,128,256]{2,1,0:T(8,128)(2,1)}, u32[]{:S(2)}, u32[]{:S(2)}) collective-permute-start(bf16[16,128,256]{2,1,0:T(8,128)(2,1)S(1)} %get-tuple-element.45.refs_3_), channel_id=1, source_target_pairs={{0,8},{4,12},{8,0},{12,4},{1,9},{5,13},{9,1},{13,5},{2,10},{6,14},... | collective-permute-start | bytes 3145736 | tf_op jit(solution)/shard_map/ppermute | solution.py:234
  88.9 83.8 %collective-permute-start.13 = (bf16[16,128,256]{2,1,0:T(8,128)(2,1)}, bf16[16,128,256]{2,1,0:T(8,128)(2,1)}, u32[]{:S(2)}, u32[]{:S(2)}) collective-permute-start(bf16[16,128,256]{2,1,0:T(8,128)(2,1)} %copy-done.16), channel_id=1, source_target_pairs={{0,12},{4,8},{8,4},{12,0},{1,13},{5,9},{9,5},{13,1},{2,14},{6,10},... | collective-permute-start | bytes 3145736 | tf_op jit(solution)/shard_map/ppermute | solution.py:234
  106.3 89.8 %collective-permute-start.15 = (bf16[16,128,256]{2,1,0:T(8,128)(2,1)}, bf16[16,128,256]{2,1,0:T(8,128)(2,1)S(1)}, u32[]{:S(2)}, u32[]{:S(2)}) collective-permute-start(bf16[16,128,256]{2,1,0:T(8,128)(2,1)} %get-tuple-element.46.refs_9_), channel_id=1, source_target_pairs={{0,8},{4,12},{8,0},{12,4},{1,9},{5,13},{9,1},{13,5},{2,10},{6,14},... | collective-permute-start | bytes 3145736 | tf_op jit(solution)/shard_map/ppermute | solution.py:234
  127.7 54.3 %collective-permute-start.14 = (bf16[16,128,256]{2,1,0:T(8,128)(2,1)}, bf16[16,128,256]{2,1,0:T(8,128)(2,1)S(1)}, u32[]{:S(2)}, u32[]{:S(2)}) collective-permute-start(bf16[16,128,256]{2,1,0:T(8,128)(2,1)} %get-tuple-element.61), channel_id=1, source_target_pairs={{0,4},{4,0},{8,12},{12,8},{1,5},{5,1},{9,13},{13,9},{2,6},{6,2},{1... | collective-permute-start | bytes 3145736 | tf_op jit(solution)/shard_map/ppermute | solution.py:234
  128.6 88.9 %collective-permute-start.16 = (bf16[16,128,256]{2,1,0:T(8,128)(2,1)}, bf16[16,128,256]{2,1,0:T(8,128)(2,1)S(1)}, u32[]{:S(2)}, u32[]{:S(2)}) collective-permute-start(bf16[16,128,256]{2,1,0:T(8,128)(2,1)} %copy-done.15), channel_id=1, source_target_pairs={{0,12},{4,8},{8,4},{12,0},{1,13},{5,9},{9,5},{13,1},{2,14},{6,10},... | collective-permute-start | bytes 3145736 | tf_op jit(solution)/shard_map/ppermute | solution.py:234
  140.8 1.0 copy-start.11
  141.8 1.0 copy-start.4
  149.2 1.0 copy-start.7
  150.2 1.0 copy-start.10
  151.2 1.0 copy-start.13
  179.0 1.0 copy-start.5
  180.0 1.0 copy-start.6
  181.0 1.0 copy-start.12
  182.0 35.5 %copy-start.27 = (bf16[16,128,256]{2,1,0:T(8,128)(2,1)}, bf16[16,128,256]{2,1,0:T(8,128)(2,1)S(1)}, u32[]{:S(2)}) copy-start(bf16[16,128,256]{2,1,0:T(8,128)(2,1)S(1)} %collective-permute-done.14.refs_1_) | copy-start | bytes 3145732
  196.1 21.4 %copy-start.26 = (bf16[16,128,256]{2,1,0:T(8,128)(2,1)}, bf16[16,128,256]{2,1,0:T(8,128)(2,1)S(1)}, u32[]{:S(2)}) copy-start(bf16[16,128,256]{2,1,0:T(8,128)(2,1)S(1)} %collective-permute-done.15.refs_2_) | copy-start | bytes 3145732
  217.5 1.0 copy-start.28
  225.0 1.1 copy-start.2
  226.0 1.0 copy-start.8
  227.0 1.0 copy-start.9
  228.0 1.0 copy-start.14
  230.9 1.6 collective-permute-start.18
  233.6 1.6 copy-start.23
  233.6 5.8 %collective-permute-start.19 = (f32[192,128]{0,1:T(8,128)S(1)}, f32[192,128]{0,1:T(8,128)S(1)}, u32[]{:S(2)}, u32[]{:S(2)}) collective-permute-start(f32[192,128]{0,1:T(8,128)S(1)} %fusion.4), channel_id=1, source_target_pairs={{0,8},{4,12},{8,0},{12,4},{1,9},{5,13},{9,1},{13,5},{2,10},{6,14},... | collective-permute-start | bytes 294920 | tf_op jit(solution)/shard_map/ppermute | solution.py:234
  240.3 1.4 collective-permute-start.20
  240.5 28.6 %collective-permute-start.24 = (bf16[16,128,256]{2,1,0:T(8,128)(2,1)}, bf16[16,128,256]{2,1,0:T(8,128)(2,1)}, u32[]{:S(2)}, u32[]{:S(2)}) collective-permute-start(bf16[16,128,256]{2,1,0:T(8,128)(2,1)} %copy-done.11), channel_id=1, source_target_pairs={{0,4},{4,0},{8,12},{12,8},{1,5},{5,1},{9,13},{13,9},{2,6},{6,2},{1... | collective-permute-start | bytes 3145736 | tf_op jit(solution)/shard_map/ppermute | solution.py:234
  241.0 28.7 %collective-permute-start.25 = (bf16[16,128,256]{2,1,0:T(8,128)(2,1)}, bf16[16,128,256]{2,1,0:T(8,128)(2,1)}, u32[]{:S(2)}, u32[]{:S(2)}) collective-permute-start(bf16[16,128,256]{2,1,0:T(8,128)(2,1)} %copy-done.13), channel_id=1, source_target_pairs={{0,4},{4,0},{8,12},{12,8},{1,5},{5,1},{9,13},{13,9},{2,6},{6,2},{1... | collective-permute-start | bytes 3145736 | tf_op jit(solution)/shard_map/ppermute | solution.py:234
  241.1 53.2 %collective-permute-start.26 = (bf16[16,128,256]{2,1,0:T(8,128)(2,1)}, bf16[16,128,256]{2,1,0:T(8,128)(2,1)}, u32[]{:S(2)}, u32[]{:S(2)}) collective-permute-start(bf16[16,128,256]{2,1,0:T(8,128)(2,1)} %copy-done.12), channel_id=1, source_target_pairs={{0,4},{4,0},{8,12},{12,8},{1,5},{5,1},{9,13},{13,9},{2,6},{6,2},{1... | collective-permute-start | bytes 3145736 | tf_op jit(solution)/shard_map/ppermute | solution.py:234
  241.5 53.6 %collective-permute-start.27 = (bf16[16,128,256]{2,1,0:T(8,128)(2,1)}, bf16[16,128,256]{2,1,0:T(8,128)(2,1)}, u32[]{:S(2)}, u32[]{:S(2)}) collective-permute-start(bf16[16,128,256]{2,1,0:T(8,128)(2,1)} %copy-done.14), channel_id=1, source_target_pairs={{0,4},{4,0},{8,12},{12,8},{1,5},{5,1},{9,13},{13,9},{2,6},{6,2},{1... | collective-permute-start | bytes 3145736 | tf_op jit(solution)/shard_map/ppermute | solution.py:234
  241.8 0.7 copy-start.24
  242.4 54.2 %collective-permute-start.28 = (bf16[16,128,256]{2,1,0:T(8,128)(2,1)}, bf16[16,128,256]{2,1,0:T(8,128)(2,1)}, u32[]{:S(2)}, u32[]{:S(2)}) collective-permute-start(bf16[16,128,256]{2,1,0:T(8,128)(2,1)} %get-tuple-element.76), channel_id=1, source_target_pairs={{0,8},{4,12},{8,0},{12,4},{1,9},{5,13},{9,1},{13,5},{2,10},{6,14},... | collective-permute-start | bytes 3145736 | tf_op jit(solution)/shard_map/ppermute | solution.py:234
  269.1 27.6 %collective-permute-start.29 = (bf16[16,128,256]{2,1,0:T(8,128)(2,1)}, bf16[16,128,256]{2,1,0:T(8,128)(2,1)}, u32[]{:S(2)}, u32[]{:S(2)}) collective-permute-start(bf16[16,128,256]{2,1,0:T(8,128)(2,1)} %get-tuple-element.77), channel_id=1, source_target_pairs={{0,12},{4,8},{8,4},{12,0},{1,13},{5,9},{9,5},{13,1},{2,14},{6,10},... | collective-permute-start | bytes 3145736 | tf_op jit(solution)/shard_map/ppermute | solution.py:234
  269.7 47.9 %collective-permute-start.30 = (bf16[16,128,256]{2,1,0:T(8,128)(2,1)}, bf16[16,128,256]{2,1,0:T(8,128)(2,1)}, u32[]{:S(2)}, u32[]{:S(2)}) collective-permute-start(bf16[16,128,256]{2,1,0:T(8,128)(2,1)} %copy-done.10), channel_id=1, source_target_pairs={{0,8},{4,12},{8,0},{12,4},{1,9},{5,13},{9,1},{13,5},{2,10},{6,14},... | collective-permute-start | bytes 3145736 | tf_op jit(solution)/shard_map/ppermute | solution.py:234
  294.3 45.4 %collective-permute-start.31 = (bf16[16,128,256]{2,1,0:T(8,128)(2,1)}, bf16[16,128,256]{2,1,0:T(8,128)(2,1)}, u32[]{:S(2)}, u32[]{:S(2)}) collective-permute-start(bf16[16,128,256]{2,1,0:T(8,128)(2,1)} %copy-done.7), channel_id=1, source_target_pairs={{0,12},{4,8},{8,4},{12,0},{1,13},{5,9},{9,5},{13,1},{2,14},{6,10},... | collective-permute-start | bytes 3145736 | tf_op jit(solution)/shard_map/ppermute | solution.py:234
  295.1 118.6 %collective-permute-start.21 = (bf16[16,128,256]{2,1,0:T(8,128)(2,1)}, bf16[16,128,256]{2,1,0:T(8,128)(2,1)}, u32[]{:S(2)}, u32[]{:S(2)}) collective-permute-start(bf16[16,128,256]{2,1,0:T(8,128)(2,1)} %copy-done.9), channel_id=1, source_target_pairs={{0,8},{4,12},{8,0},{12,4},{1,9},{5,13},{9,1},{13,5},{2,10},{6,14},... | collective-permute-start | bytes 3145736 | tf_op jit(solution)/shard_map/ppermute | solution.py:234
  296.6 114.0 %collective-permute-start.22 = (bf16[16,128,256]{2,1,0:T(8,128)(2,1)}, bf16[16,128,256]{2,1,0:T(8,128)(2,1)}, u32[]{:S(2)}, u32[]{:S(2)}) collective-permute-start(bf16[16,128,256]{2,1,0:T(8,128)(2,1)} %copy-done.5), channel_id=1, source_target_pairs={{0,12},{4,8},{8,4},{12,0},{1,13},{5,9},{9,5},{13,1},{2,14},{6,10},... | collective-permute-start | bytes 3145736 | tf_op jit(solution)/shard_map/ppermute | solution.py:234
  296.8 110.7 %collective-permute-start.23 = (bf16[16,128,256]{2,1,0:T(8,128)(2,1)}, bf16[16,128,256]{2,1,0:T(8,128)(2,1)}, u32[]{:S(2)}, u32[]{:S(2)}) collective-permute-start(bf16[16,128,256]{2,1,0:T(8,128)(2,1)} %copy-done.6), channel_id=1, source_target_pairs={{0,8},{4,12},{8,0},{12,4},{1,9},{5,13},{9,1},{13,5},{2,10},{6,14},... | collective-permute-start | bytes 3145736 | tf_op jit(solution)/shard_map/ppermute | solution.py:234
  317.6 111.9 %collective-permute-start.17 = (bf16[16,128,256]{2,1,0:T(8,128)(2,1)}, bf16[16,128,256]{2,1,0:T(8,128)(2,1)S(1)}, u32[]{:S(2)}, u32[]{:S(2)}) collective-permute-start(bf16[16,128,256]{2,1,0:T(8,128)(2,1)} %copy-done.8), channel_id=1, source_target_pairs={{0,12},{4,8},{8,4},{12,0},{1,13},{5,9},{9,5},{13,1},{2,14},{6,10},... | collective-permute-start | bytes 3145736 | tf_op jit(solution)/shard_map/ppermute | solution.py:234
